TPU v7x, 512 devices: a whole 4x8x8 slice. The times are simulated.
512 devices in a mesh: plant: 8 (over z), feat: 8 (over x, core), samp: 8 (over y).
Axes of the slice: x: 4, y: 8, z: 8, core: 2. Of those that a mesh axis runs over, the one named last changes fastest.
Arguments:
- embeddings: bfloat16 [32768, 4096], P(('plant', 'samp'), 'feat'), may hold values from -6 to 6
- plant_ids: int32 [32768, 1], P(('plant', 'samp')), may hold values from 0 to 7; in each aligned block of 512 rows (0 to 511, 512 to 1023, ...) at most 128 rows name the same one
- labels: int32 [32768], P(('plant', 'samp')), may hold values from 0 to 1
- weights: float32 [8, 4096], P('plant', 'feat'), may hold values from -0.09375 to 0.09375
Outputs:
- newton_step: float32 [8, 4096], P('plant', ('feat', 'samp'))
- gradient: float32 [8, 4096], P('plant', ('feat', 'samp'))
Inputs may be any that keep to these rules, and one draw needn't show every extreme that they name: `plant_ids`: in the 512 rows of one device no plant is named by more than 128 rows, a bound that some block reaches; every plant is named by some row.
All inputs are finite; a program needn't handle non-finite values.
Results may differ from a plain program's by a relative error of at most 0.0034.
Values may be sent and summed in bfloat16 or wider, within the bound.
No kernel may reach another device: no remote copies, remote signals or barrier semaphores. Data moves between devices by JAX's collectives and lax.ppermute only.
A program may use at most 64 MiB of HBM per device.

v0:
```python
import jax
import jax.numpy as jnp
from jax import lax
from jax.sharding import PartitionSpec as P

ITERS = 2


penalty = 0.1


def feat_total(values):
    return lax.psum(values, "feat")


def inner(first, second):
    return lax.psum(jnp.sum(first * second), ("feat", "samp"))


def shards(embeddings, plant_ids, labels, weights):
    plants = lax.axis_size("plant")
    samps = lax.axis_size("samp")
    rows_here, width_here = embeddings.shape
    share = width_here // samps
    own_samp = lax.axis_index("samp")
    plant_col = plant_ids[:, 0]
    members = (plant_col[:, None] == jnp.arange(plants, dtype=jnp.int32)[None, :]).astype(jnp.int32)
    weight_share = lax.dynamic_slice_in_dim(weights, own_samp * share, share, 1)
    most_rows = 2 * rows_here // plants
    capacity = most_rows // samps
    before = jnp.cumsum(members, axis=0) - members
    ranking = jnp.sum(before * members, axis=1)
    slot_index = (plant_col * samps + ranking % samps) * capacity + ranking // samps
    slots_all = plants * samps * capacity
    send_rows = jnp.zeros((slots_all, width_here), jnp.bfloat16).at[slot_index].set(embeddings)
    send_tags = jnp.zeros((slots_all,), jnp.int32).at[slot_index].set(labels + 1)
    recv_rows, recv_tags = (
        lax.all_to_all(
            send_rows.reshape(plants * samps, capacity, width_here),
            ("plant", "samp"),
            split_axis=0,
            concat_axis=0,
            tiled=True,
        ),
        lax.all_to_all(
            send_tags.reshape(plants * samps, capacity),
            ("plant", "samp"),
            split_axis=0,
            concat_axis=0,
            tiled=True,
        ),
    )
    grouped = recv_rows.reshape(slots_all, width_here)
    tag_vals = recv_tags.reshape(slots_all)
    valid_rows = tag_vals > 0
    targets = jnp.maximum(tag_vals - 1, 0).astype(jnp.float32)
    count = lax.psum(jnp.sum(valid_rows.astype(jnp.float32)), "samp")
    logits = feat_total(
        jnp.dot(grouped, weights[0].astype(jnp.bfloat16), preferred_element_type=jnp.float32)
    )
    prob_vals = jax.nn.sigmoid(logits)
    residual = jnp.where(valid_rows, prob_vals - targets, 0.0)
    curvature = jnp.where(valid_rows, prob_vals * (1.0 - prob_vals), 0.0)

    def spread(row_vals):
        columns = jnp.dot(row_vals, grouped, preferred_element_type=jnp.float32)
        return lax.psum_scatter(
            columns.reshape(samps, share), "samp", scatter_dimension=0, tiled=True
        )

    gradient = spread(residual.astype(jnp.bfloat16)) / count + penalty * weight_share
    newton_step = jnp.zeros_like(gradient)
    resid_vec = -gradient
    direction = resid_vec
    sq_norm = inner(resid_vec, resid_vec)
    for iteration in range(ITERS):
        dir_bf = direction.astype(jnp.bfloat16)
        full_dir = lax.all_gather(dir_bf, "samp", axis=1, tiled=True)
        projected = feat_total(jnp.dot(grouped, full_dir[0], preferred_element_type=jnp.float32))
        curv_image = (
            spread((curvature * projected).astype(jnp.bfloat16)) / count + penalty * direction
        )
        step_len = sq_norm / inner(direction, curv_image)
        newton_step = newton_step + step_len * direction
        if iteration + 1 < ITERS:
            resid_vec = resid_vec - step_len * curv_image
            sq_next = inner(resid_vec, resid_vec)
            direction = resid_vec + sq_next / sq_norm * direction
            sq_norm = sq_next
    return (newton_step, gradient)


def solution(mesh):
    placed = (
        P(("plant", "samp"), "feat"),
        P(("plant", "samp"), None),
        P(("plant", "samp")),
        P("plant", "feat"),
    )
    return jax.shard_map(
        shards,
        mesh=mesh,
        in_specs=placed,
        out_specs=(P("plant", ("feat", "samp")), P("plant", ("feat", "samp"))),
        check_vma=False,
    )
```

profile of v0, /device:TPU:1, one launch (start us, length us, event | category | flops | bytes accessed | tf_op | source)
XLA Modules:
  0.0 567.6 jit_solution(9045763791688096667)
XLA Ops:
  0.6 0.7 fusion.5
  1.3 1.1 reduce-window.6
  2.4 0.2 slice_reduce_fusion
  2.7 0.0 copy-start
  2.7 0.7 copy-done
  3.4 0.1 fusion.4
  3.5 0.0 copy-start.3
  3.5 0.6 copy-done.3
  4.2 2.4 scatter_custom_fusion
  6.6 0.7 all_to_all.9
  7.3 17.1 %all-to-all-start = ((s32[64,1,16]{2,1,0:T(1,128)}), s32[64,1,16]{2,1,0:T(1,128)S(1)}, u32[]{:S(2)}, u32[]{:S(2)}) async-start(s32[64,1,16]{2,1,0:T(1,128)} %bitcast.6), calls=%async_computation | async-start | bytes 65536 | tf_op jit(solution)/shard_map/all_to_all | solution.py:45
  24.4 4.0 scatter_custom_fusion.1
  28.4 6.8 %all-to-all-done = s32[64,1,16]{2,1,0:T(1,128)S(1)} async-done(((s32[64,1,16]{2,1,0:T(1,128)}), s32[64,1,16]{2,1,0:T(1,128)S(1)}, u32[]{:S(2)}, u32[]{:S(2)}) %all-to-all-start) | async-done | bytes 4128 | tf_op jit(solution)/shard_map/all_to_all | solution.py:45
  35.3 5.3 all-to-all-start.1
  40.6 0.0 copy-start.4
  40.6 0.7 copy-done.4
  41.2 0.7 fusion.15
  42.6 0.1 compare_reduce_fusion
  42.7 0.1 gt.9
  42.8 0.8 fusion.2
  43.5 0.0 copy-start.2
  43.5 0.1 convert_element_type.44
  43.6 23.6 %all-to-all-done.1 = bf16[64,16,512]{2,1,0:T(8,128)(2,1)S(1)} async-done(((bf16[64,16,512]{2,1,0:T(8,128)(2,1)}), bf16[64,16,512]{2,1,0:T(8,128)(2,1)S(1)}, u32[]{:S(2)}, u32[]{:S(2)}) %all-to-all-start.1) | async-done | bytes 1048608 | tf_op jit(solution)/shard_map/all_to_all | solution.py:38
  67.2 0.0 copy-done.2
  67.2 0.4 fusion.8
  67.5 15.9 %psum.56 = f32[1024]{0:T(1024)S(1)} all-reduce(f32[1024]{0:T(1024)S(1)} %bitcast.61), channel_id=1, replica_groups=mesh['plant'=8,'feat'=8,'samp'=8] {'feat'}, use_global_device_ids=true, to_apply=%region_5.6 | all-reduce | flops 1024 | bytes 8192 | tf_op jit(solution)/shard_map/psum | solution.py:13
  83.5 0.5 copy.9
  84.0 0.5 fusion.16
  84.6 13.0 %all-reduce.6 = (f32[8,64]{1,0:T(8,128)S(1)}, f32[]{:T(128)}) all-reduce(f32[8,64]{1,0:T(8,128)S(1)} %bitcast.56, f32[]{:T(128)} %get-tuple-element.2), channel_id=2, replica_groups=mesh['plant'=8,'feat'=8,'samp'=8] {'samp'}, use_global_device_ids=true, to_apply=%region_6.7.clone | all-reduce | flops 513 | bytes 4104
  97.5 1.4 convert_bitcast_fusion.1
  99.0 0.0 copy-start.1
  99.0 0.2 dynamic-update-slice
  99.2 11.2 %all-reduce = bf16[512]{0:T(512)(128)(2,1)S(1)} all-reduce(bf16[512]{0:T(512)(128)(2,1)S(1)} %dynamic-update-slice), channel_id=1, replica_groups=mesh['plant'=8,'feat'=8,'samp'=8] {'samp'}, use_global_device_ids=true, to_apply=%add | all-reduce | flops 512 | bytes 2048 | tf_op jit(solution)/shard_map/squeeze | solution.py:79
  110.4 0.4 fusion.17
  110.7 19.4 %psum.59 = f32[1024]{0:T(1024)S(1)} all-reduce(f32[1024]{0:T(1024)S(1)} %bitcast.59), channel_id=1, replica_groups=mesh['plant'=8,'feat'=8,'samp'=8] {'feat'}, use_global_device_ids=true, to_apply=%region_11.12 | all-reduce | flops 1024 | bytes 8192 | tf_op jit(solution)/shard_map/psum | solution.py:13
  130.2 0.5 fusion.18
  130.7 12.8 %all-reduce.3 = f32[8,64]{1,0:T(8,128)S(1)} all-reduce(f32[8,64]{1,0:T(8,128)S(1)} %bitcast.60), channel_id=3, replica_groups=mesh['plant'=8,'feat'=8,'samp'=8] {'samp'}, use_global_device_ids=true, to_apply=%region_12.13.clone | all-reduce | flops 512 | bytes 4096
  143.5 2.0 multiply_reduce_fusion.1
  145.5 119.7 %all-reduce.5 = (f32[]{:T(128)}, f32[]{:T(128)}) all-reduce(f32[]{:T(128)} %get-tuple-element.5, f32[]{:T(128)} %get-tuple-element.4), channel_id=1, replica_groups=mesh['plant'=8,'feat'=8,'samp'=8] {'feat','samp'}, use_global_device_ids=true, to_apply=%region_10.11 | all-reduce | flops 2 | bytes 16 | tf_op jit(solution)/shard_map/psum | solution.py:17
  266.6 0.6 multiply_reduce_fusion
  267.2 126.8 %psum.61 = f32[]{:T(128)} all-reduce(f32[]{:T(128)} %multiply_reduce_fusion), channel_id=1, replica_groups=mesh['plant'=8,'feat'=8,'samp'=8] {'feat','samp'}, use_global_device_ids=true, to_apply=%region_16.17 | all-reduce | flops 1 | bytes 8 | tf_op jit(solution)/shard_map/psum | solution.py:17
  395.3 0.2 dynamic-update-slice.1
  395.6 10.8 %all-reduce.1 = bf16[512]{0:T(512)(128)(2,1)S(1)} all-reduce(bf16[512]{0:T(512)(128)(2,1)S(1)} %dynamic-update-slice.1), channel_id=1, replica_groups=mesh['plant'=8,'feat'=8,'samp'=8] {'samp'}, use_global_device_ids=true, to_apply=%add.1 | all-reduce | flops 512 | bytes 2048 | tf_op jit(solution)/shard_map/squeeze | solution.py:79
  406.4 0.4 fusion.19
  406.8 24.1 %psum.62 = f32[1024]{0:T(1024)S(1)} all-reduce(f32[1024]{0:T(1024)S(1)} %bitcast.57), channel_id=1, replica_groups=mesh['plant'=8,'feat'=8,'samp'=8] {'feat'}, use_global_device_ids=true, to_apply=%region_17.18 | all-reduce | flops 1024 | bytes 8192 | tf_op jit(solution)/shard_map/psum | solution.py:13
  430.9 0.5 fusion.20
  431.4 12.4 %all-reduce.4 = f32[8,64]{1,0:T(8,128)S(1)} all-reduce(f32[8,64]{1,0:T(8,128)S(1)} %bitcast.58), channel_id=4, replica_groups=mesh['plant'=8,'feat'=8,'samp'=8] {'samp'}, use_global_device_ids=true, to_apply=%region_18.19.clone | all-reduce | flops 512 | bytes 4096
  443.8 2.0 fusion.14
  445.9 120.0 %psum.63 = f32[]{:T(128)} all-reduce(f32[]{:T(128)} %fusion.14), channel_id=1, replica_groups=mesh['plant'=8,'feat'=8,'samp'=8] {'feat','samp'}, use_global_device_ids=true, to_apply=%region_20.21 | all-reduce | flops 1 | bytes 8 | tf_op jit(solution)/shard_map/psum | solution.py:17
  567.1 0.0 copy-done.1
  567.1 0.5 multiply_add_fusion
  (15 shorter events, 0.2 us)
Async XLA Ops:
  2.7 0.7 copy-start
  3.5 0.7 copy-start.3
  7.3 28.0 %all-to-all-start = ((s32[64,1,16]{2,1,0:T(1,128)}), s32[64,1,16]{2,1,0:T(1,128)S(1)}, u32[]{:S(2)}, u32[]{:S(2)}) async-start(s32[64,1,16]{2,1,0:T(1,128)} %bitcast.6), calls=%async_computation | async-start | bytes 65536 | tf_op jit(solution)/shard_map/all_to_all | solution.py:45
  35.3 31.9 %all-to-all-start.1 = ((bf16[64,16,512]{2,1,0:T(8,128)(2,1)}), bf16[64,16,512]{2,1,0:T(8,128)(2,1)S(1)}, u32[]{:S(2)}, u32[]{:S(2)}) async-start(bf16[64,16,512]{2,1,0:T(8,128)(2,1)} %bitcast.7), calls=%async_computation.1 | async-start | bytes 2097152 | tf_op jit(solution)/shard_map/all_to_all | solution.py:38
  40.6 0.7 copy-start.4
  43.5 23.7 %copy-start.2 = (f32[1,512]{1,0:T(1,128)S(1)}, f32[1,512]{1,0:T(1,128)}, u32[]{:S(2)}) copy-start(f32[1,512]{1,0:T(1,128)} %param.7) | copy-start | bytes 6148
  99.0 468.1 %copy-start.1 = (f32[1,64]{1,0:T(1,128)}, f32[1,64]{1,0:T(1,128)S(1)}, u32[]{:S(2)}) copy-start(f32[1,64]{1,0:T(1,128)S(1)} %get-tuple-element.14) | copy-start | bytes 772
where the time goes:
time: 577 us; the launch traced here: 568 us
  blocking collectives  486 us (84%)
  waiting for transfers between devices  30.4 us (5%)
  starting transfers between devices  22.4 us (4%)
  local copies, waits for them, and re-layouts  11.2 us (2%)
  other arithmetic  9.4 us (2%)
    psum x3, blocking collectives, inner(): return lax.psum(jnp.sum(first * second), ('feat', 'samp'))  367 us
    psum x3, blocking collectives, feat_total(): return lax.psum(values, 'feat')  59.5 us
    unnamed x3, blocking collectives  38.2 us
    all_to_all x1, waiting for transfers between devices, shards(): lax.all_to_all(send_rows.reshape(plants * samps, capacity, width_here), (...  23.6 us
    squeeze x2, blocking collectives, shards(): full_dir[0]  22 us
    all_to_all x1, starting transfers between devices, shards(): lax.all_to_all(send_tags.reshape(plants * samps, capacity), ('plant', 'sa...  17.1 us
  transfers between devices with their start and end apart: 2, of which 2 were waited for; matrix products, arithmetic and copies ran while one was open for 1% of the time, Pallas kernels for 0%

commit v1 on v0

v1 whole, which is shorter than its diff:
```python
import functools

import jax
import jax.numpy as jnp
from jax import lax
from jax.experimental import pallas as pl
from jax.experimental.pallas import tpu as pltpu
from jax.sharding import PartitionSpec as P

penalty = 0.1
PEERS = 8
LANES = 128
f32 = jnp.float32
bf16 = jnp.bfloat16


def nt(a, b):
    return lax.dot_general(a, b, (((1,), (1,)), ((), ())), preferred_element_type=f32)


def nn(a, b):
    return lax.dot_general(a, b, (((1,), (0,)), ((), ())), preferred_element_type=f32)


def rep(row):
    return jnp.broadcast_to(row, (PEERS, row.shape[1]))


def lane0(ref, at):
    return jnp.sum(ref[:, at : at + LANES], axis=0, keepdims=True)[:, :1]


def call(kernel, *args, out):
    return pl.pallas_call(
        kernel,
        out_shape=out,
        in_specs=[pl.BlockSpec(memory_space=pltpu.VMEM)] * len(args),
        out_specs=jax.tree.map(lambda _: pl.BlockSpec(memory_space=pltpu.VMEM), out),
        name=kernel.func.__name__ if isinstance(kernel, functools.partial) else kernel.__name__,
    )(*args)


def shape(*dims, dtype=f32):
    return jax.ShapeDtypeStruct(dims, dtype)


def pack_rows(cap, ids_ref, lab_ref, emb_ref, out_ref):
    rows = emb_ref.shape[0]
    ids = ids_ref[...]
    heads = lax.broadcasted_iota(jnp.int32, (PEERS, rows), 0)
    members = heads == ids
    mem_f = members.astype(f32)
    earlier = lax.broadcasted_iota(jnp.int32, (rows, rows), 0) < lax.broadcasted_iota(
        jnp.int32, (rows, rows), 1
    )
    before = nn(mem_f.astype(bf16), earlier.astype(f32).astype(bf16))
    rank = jnp.sum(before * mem_f, axis=0, keepdims=True).astype(jnp.int32)
    at_rank = lax.broadcasted_iota(jnp.int32, (cap, rows), 0) == rank
    tags = (lab_ref[...] + 1).astype(f32)
    tag_slots = nt((mem_f * tags).astype(bf16), at_rank.astype(f32).astype(bf16))
    emb = emb_ref[...]
    for p in range(PEERS):
        pick = (at_rank & (ids == p)).astype(f32).astype(bf16)
        out_ref[p, :cap, :] = nn(pick, emb).astype(bf16)
        out_ref[p, cap:, :cap] = jnp.broadcast_to(tag_slots[p : p + 1], (PEERS, cap)).astype(bf16)
        out_ref[p, cap:, cap:] = jnp.zeros((PEERS, rows - cap), bf16)


def take_rows(cap, got_ref, w_ref, rows_ref, tags_ref, out_ref):
    for p in range(PEERS):
        rows_ref[p * cap : (p + 1) * cap, :] = got_ref[p, :cap, :]
        tags_ref[:, p * cap : (p + 1) * cap] = got_ref[p, cap:, :cap].astype(f32)
    out_ref[...] = nt(rep(w_ref[...]).astype(bf16), rows_ref[...])


def to_residual(got_ref, tags_ref, rows_ref, curv_ref, out_ref):
    width = rows_ref.shape[1]
    logits = jnp.sum(got_ref[...], axis=0, keepdims=True)
    tags = tags_ref[0:1, :]
    valid = tags > 0.0
    prob = jax.nn.sigmoid(logits)
    residual = jnp.where(valid, prob - jnp.maximum(tags - 1.0, 0.0), 0.0)
    curv_ref[...] = rep(jnp.where(valid, prob * (1.0 - prob), 0.0))
    out_ref[:, :width] = nn(rep(residual).astype(bf16), rows_ref[...])
    count = jnp.sum(valid.astype(f32), axis=1, keepdims=True)
    out_ref[:, width:] = jnp.broadcast_to(count, (PEERS, LANES))


def to_direction(got_ref, w_ref, rows_ref, grad_ref, count_ref, out_ref):
    width, slots = rows_ref.shape[1], rows_ref.shape[0]
    count = lane0(got_ref, width)
    grad = jnp.sum(got_ref[:, :width], axis=0, keepdims=True) / count + penalty * w_ref[...]
    grad_ref[...] = grad
    count_ref[...] = jnp.broadcast_to(count, (1, LANES))
    out_ref[:, :slots] = nt(rep(-grad).astype(bf16), rows_ref[...])
    out_ref[:, slots:] = jnp.broadcast_to(
        jnp.sum(grad * grad, axis=1, keepdims=True), (PEERS, LANES)
    )


def to_image(got_ref, curv_ref, rows_ref, proj_ref, out_ref):
    width, slots = rows_ref.shape[1], rows_ref.shape[0]
    total = jnp.sum(got_ref[...], axis=0, keepdims=True)
    proj_ref[...] = total
    proj = total[:, :slots]
    weighted = (curv_ref[0:1, :] * proj).astype(bf16)
    out_ref[:, :width] = nn(rep(weighted.astype(f32)).astype(bf16), rows_ref[...])
    bent = jnp.sum(weighted.astype(f32) * proj, axis=1, keepdims=True)
    out_ref[:, width:] = jnp.broadcast_to(bent, (PEERS, LANES))


def to_second(got_ref, proj_ref, grad_ref, count_ref, rows_ref, keep_ref, out_ref):
    width, slots = rows_ref.shape[1], rows_ref.shape[0]
    count = count_ref[:, :1]
    sq_norm = proj_ref[:, slots : slots + 1]
    direction = -grad_ref[...]
    image = jnp.sum(got_ref[:, :width], axis=0, keepdims=True) / count + penalty * direction
    step = sq_norm / (lane0(got_ref, width) / count + penalty * sq_norm)
    resid = direction - step * image
    keep_ref[:, :width] = resid
    keep_ref[:, width:] = jnp.broadcast_to(step, (1, LANES))
    out_ref[:, :slots] = nt(rep(resid).astype(bf16), rows_ref[...])
    out_ref[:, slots : slots + LANES] = jnp.broadcast_to(
        jnp.sum(resid * resid, axis=1, keepdims=True), (PEERS, LANES)
    )
    out_ref[:, slots + LANES :] = jnp.broadcast_to(
        jnp.sum(resid * direction, axis=1, keepdims=True), (PEERS, LANES)
    )


def to_bend(got_ref, proj_ref, curv_ref, keep_ref, out_ref):
    slots = curv_ref.shape[1]
    total = jnp.sum(got_ref[...], axis=0, keepdims=True)
    sq_norm = proj_ref[:, slots : slots + 1]
    sq_next = total[:, slots : slots + 1]
    cross = total[:, slots + LANES : slots + LANES + 1]
    beta = sq_next / sq_norm
    proj = total[:, :slots] + beta * proj_ref[:, :slots]
    weighted = (curv_ref[0:1, :] * proj).astype(bf16).astype(f32)
    out_ref[...] = jnp.broadcast_to(
        jnp.sum(weighted * proj, axis=1, keepdims=True), (PEERS, LANES)
    )
    dir_sq = sq_next + 2.0 * beta * cross + beta * beta * sq_norm
    keep_ref[0:1, :] = jnp.broadcast_to(beta, (1, LANES))
    keep_ref[1:2, :] = jnp.broadcast_to(sq_next, (1, LANES))
    keep_ref[2:3, :] = jnp.broadcast_to(dir_sq, (1, LANES))
    keep_ref[3:, :] = jnp.zeros((PEERS - 3, LANES), f32)


def to_step(got_ref, count_ref, keep_ref, first_ref, grad_ref, resid_ref, out_ref):
    beta, sq_next, dir_sq = keep_ref[0:1, :1], keep_ref[1:2, :1], keep_ref[2:3, :1]
    step = sq_next / (lane0(got_ref, 0) / count_ref[:, :1] + penalty * dir_sq)
    direction = -grad_ref[...]
    out_ref[...] = first_ref[:, :1] * direction + step * (resid_ref[...] + beta * direction)


def exchange(values, axis):
    return lax.all_to_all(values, axis, split_axis=0, concat_axis=0, tiled=True)


def shards(embeddings, plant_ids, labels, weights):
    rows_here, width = embeddings.shape
    samps = lax.axis_size("samp")
    share = width // samps
    cap = 2 * rows_here // PEERS
    slots = PEERS * cap
    at = lax.axis_index("samp") * share

    sent = call(
        functools.partial(pack_rows, cap),
        plant_ids.reshape(1, rows_here),
        labels.reshape(1, rows_here),
        embeddings,
        out=shape(PEERS, cap + PEERS, width, dtype=bf16),
    )
    got = exchange(sent, "plant")
    rows, tags, part = call(
        functools.partial(take_rows, cap),
        got,
        weights,
        out=(shape(slots, width, dtype=bf16), shape(PEERS, slots), shape(PEERS, slots)),
    )
    got = exchange(part, "feat")
    curv, part = call(
        to_residual, got, tags, rows, out=(shape(PEERS, slots), shape(PEERS, width + LANES))
    )
    got = exchange(part, "samp")
    grad, count, part = call(
        to_direction,
        got,
        weights,
        rows,
        out=(shape(1, width), shape(1, LANES), shape(PEERS, slots + LANES)),
    )
    got = exchange(part, "feat")
    proj, part = call(
        to_image, got, curv, rows, out=(shape(1, slots + LANES), shape(PEERS, width + LANES))
    )
    got = exchange(part, "samp")
    kept, part = call(
        to_second,
        got,
        proj,
        grad,
        count,
        rows,
        out=(shape(1, width + LANES), shape(PEERS, slots + 2 * LANES)),
    )
    got = exchange(part, "feat")
    scalars, part = call(
        to_bend, got, proj, curv, out=(shape(PEERS, LANES), shape(PEERS, LANES))
    )
    got = exchange(part, "samp")
    grad_share = lax.dynamic_slice_in_dim(grad, at, share, 1)
    resid_share = lax.dynamic_slice_in_dim(kept, at, share, 1)
    newton_step = call(
        to_step,
        got,
        count,
        scalars,
        kept[:, width:],
        grad_share,
        resid_share,
        out=shape(1, share),
    )
    return newton_step, grad_share


def solution(mesh):
    placed = (
        P(("plant", "samp"), "feat"),
        P(("plant", "samp"), None),
        P(("plant", "samp")),
        P("plant", "feat"),
    )
    return jax.shard_map(
        shards,
        mesh=mesh,
        in_specs=placed,
        out_specs=(P("plant", ("feat", "samp")), P("plant", ("feat", "samp"))),
        check_vma=False,
    )
```

time: 577 us -> 130 us (0.23); the launches traced: 568 us -> 129 us
  blocking collectives: 486 us -> 73.4 us
  Pallas kernels: 0 us -> 17.1 us
  waiting for transfers between devices: 30.4 us -> 14.1 us
  starting transfers between devices: 22.4 us -> 11.7 us
  other arithmetic: 9.4 us -> 0 us
    psum x6 -> x0, blocking collectives: 426 us -> none  [the longest x3 367 us: inner(): return lax.psum(jnp.sum(first * second), ('feat', 'samp'))]
    all_to_all x0 -> x4, blocking collectives: none -> 73.4 us  [exchange(): return lax.all_to_all(values, axis, split_axis=0, concat_axis=0, tiled=True)]
    unnamed x3 -> x0, blocking collectives: 38.2 us -> none
    squeeze x2 -> x0, blocking collectives: 22 us -> none  [shards(): full_dir[0]]
    pallas_call x0 -> x8, Pallas kernels: none -> 17.1 us  [call(): pl.pallas_call(kernel, out_shape=out, in_specs=[pl.BlockSpec(memory_space...]
    all_to_all x2 -> x3, waiting for transfers between devices: 30.4 us -> 14.1 us  [exchange(): return lax.all_to_all(values, axis, split_axis=0, concat_axis=0, tiled=True)]
    all_to_all x2 -> x3, starting transfers between devices: 22.4 us -> 11.7 us  [exchange(): return lax.all_to_all(values, axis, split_axis=0, concat_axis=0, tiled=True)]
    scatter x2 -> x0, local copies, waits for them, and re-layouts: 6.41 us -> none  [the longest x1 3.97 us: shards(): jnp.zeros((slots_all, width_here), jnp.bfloat16).at[slot_index]]
  transfers between devices with their start and end apart: 2 -> 3, of which waited for: 2 -> 3; matrix products, arithmetic and copies ran while one was open for 1% -> 3% of each run, Pallas kernels for 0% -> 0%
where the time goes in v1:
time: 130 us; the launch traced here: 129 us
  blocking collectives  73.4 us (56%)
  Pallas kernels  17.1 us (13%)
  waiting for transfers between devices  14.1 us (11%)
  local copies, waits for them, and re-layouts  12.4 us (10%)
  starting transfers between devices  11.7 us (9%)
    all_to_all x4, blocking collectives, exchange(): return lax.all_to_all(values, axis, split_axis=0, concat_axis=0, tiled=True)  73.4 us
    pallas_call x8, Pallas kernels, call(): pl.pallas_call(kernel, out_shape=out, in_specs=[pl.BlockSpec(memory_space...  17.1 us
    all_to_all x3, waiting for transfers between devices, exchange(): return lax.all_to_all(values, axis, split_axis=0, concat_axis=0, tiled=True)  14.1 us
    all_to_all x3, starting transfers between devices, exchange(): return lax.all_to_all(values, axis, split_axis=0, concat_axis=0, tiled=True)  11.7 us
    all_to_all x5, local copies, waits for them, and re-layouts, exchange(): return lax.all_to_all(values, axis, split_axis=0, concat_axis=0, tiled=True)  5.12 us
    unnamed x7, local copies, waits for them, and re-layouts  3.64 us
  transfers between devices with their start and end apart: 3, of which 3 were waited for; matrix products, arithmetic and copies ran while one was open for 3% of the time, Pallas kernels for 0%

profile of v1, /device:TPU:1, one launch (start us, length us, event | category | flops | bytes accessed | tf_op | source)
XLA Modules:
  0.0 129.5 jit_solution(9566941945083007460)
XLA Ops:
  0.6 3.0 %pack_rows.1 = bf16[8,136,512]{2,1,0:T(8,128)(2,1)} custom-call(s32[1,512]{1,0:T(1,128)} %bitcast.38, s32[1,512]{1,0:T(1,128)} %bitcast.39, bf16[512,512]{1,0:T(8,128)(2,1)} %emb_ref.1), custom_call_target="tpu_custom_call" | custom-call | tf_op jit(solution)/shard_map/pack_rows/pallas_call | solution.py:34
  3.6 39.6 %all_to_all.71.got_ref = bf16[8,136,512]{2,1,0:T(8,128)(2,1)} all-to-all(bf16[8,136,512]{2,1,0:T(8,128)(2,1)} %pack_rows.1), channel_id=1, replica_groups=mesh['plant'=8,'feat'=8,'samp'=8] {'plant'}, dimensions={0} | all-to-all | bytes 2228224 | tf_op jit(solution)/shard_map/all_to_all | solution.py:158
  43.2 2.5 %take_rows.1 = (bf16[1024,512]{1,0:T(8,128)(2,1)}, f32[8,1024]{1,0:T(8,128)}, f32[8,1024]{1,0:T(8,128)}) custom-call(bf16[8,136,512]{2,1,0:T(8,128)(2,1)} %all_to_all.71.got_ref, f32[1,512]{1,0:T(1,128)} %w_ref.3), custom_call_target="tpu_custom_call" | custom-call | tf_op jit(solution)/shard_map/take_rows/pallas_call | solution.py:34
  45.6 0.8 copy.6
  46.4 11.3 %all_to_all.72 = f32[8,1,1024]{2,1,0:T(1,128)S(1)} all-to-all(f32[8,1,1024]{2,1,0:T(1,128)S(1)} %copy.6), channel_id=1, replica_groups=mesh['plant'=8,'feat'=8,'samp'=8] {'feat'}, dimensions={0} | all-to-all | bytes 65536 | tf_op jit(solution)/shard_map/all_to_all | solution.py:158
  57.7 0.6 copy.24
  58.4 2.1 %to_residual.1 = (f32[8,1024]{1,0:T(8,128)}, f32[8,640]{1,0:T(8,128)}) custom-call(f32[8,1024]{1,0:T(8,128)} %bitcast.28, f32[8,1024]{1,0:T(8,128)} %get-tuple-element.17.tags_ref, bf16[1024,512]{1,0:T(8,128)(2,1)} %get-tuple-element.18.rows_ref), custom_call_target="tpu_custom_call" | custom-call | tf_op jit(solution)/shard_map/to_residual/pallas_call | solution.py:34
  60.5 0.7 copy.7
  61.3 13.3 %all_to_all.73 = f32[8,1,640]{2,1,0:T(1,128)S(1)} all-to-all(f32[8,1,640]{2,1,0:T(1,128)S(1)} %copy.7), channel_id=1, replica_groups=mesh['plant'=8,'feat'=8,'samp'=8] {'samp'}, dimensions={0} | all-to-all | bytes 40960 | tf_op jit(solution)/shard_map/all_to_all | solution.py:158
  74.5 0.6 copy.26
  75.1 2.3 %to_direction.1 = (f32[1,512]{1,0:T(1,128)}, f32[1,128]{1,0:T(1,128)}, f32[8,1152]{1,0:T(8,128)}) custom-call(f32[8,640]{1,0:T(8,128)} %bitcast.30, f32[1,512]{1,0:T(1,128)} %w_ref.3, bf16[1024,512]{1,0:T(8,128)(2,1)} %get-tuple-element.18.rows_ref), custom_call_target="tpu_custom_call" | custom-call | tf_op jit(solution)/shard_map/to_direction/pallas_call | solution.py:34
  77.4 0.8 copy.8
  78.2 9.3 %all_to_all.74 = f32[8,1,1152]{2,1,0:T(1,128)S(1)} all-to-all(f32[8,1,1152]{2,1,0:T(1,128)S(1)} %copy.8), channel_id=1, replica_groups=mesh['plant'=8,'feat'=8,'samp'=8] {'feat'}, dimensions={0} | all-to-all | bytes 73728 | tf_op jit(solution)/shard_map/all_to_all | solution.py:158
  87.5 0.6 copy.23
  88.1 2.1 %to_image.1 = (f32[1,1152]{1,0:T(1,128)}, f32[8,640]{1,0:T(8,128)}) custom-call(f32[8,1152]{1,0:T(8,128)} %bitcast.27, f32[8,1024]{1,0:T(8,128)} %get-tuple-element.21.curv_ref, bf16[1024,512]{1,0:T(8,128)(2,1)} %get-tuple-element.18.rows_ref), custom_call_target="tpu_custom_call" | custom-call | tf_op jit(solution)/shard_map/to_image/pallas_call | solution.py:34
  90.2 1.3 %copy.9 = f32[8,1,640]{2,1,0:T(1,128)} copy(f32[8,1,640]{2,0,1:T(8,128)} %bitcast.35) | data formatting | bytes 40960 | tf_op jit(solution)/shard_map/all_to_all | solution.py:158
  91.5 3.3 %all-to-all-start.4 = ((f32[8,1,640]{2,1,0:T(1,128)}), f32[8,1,640]{2,1,0:T(1,128)S(1)}, u32[]{:S(2)}, u32[]{:S(2)}) async-start(f32[8,1,640]{2,1,0:T(1,128)} %copy.9), calls=%async_computation.4 | async-start | bytes 40960 | tf_op jit(solution)/shard_map/all_to_all | solution.py:158
  94.9 6.6 %all-to-all-done.4 = f32[8,1,640]{2,1,0:T(1,128)S(1)} async-done(((f32[8,1,640]{2,1,0:T(1,128)}), f32[8,1,640]{2,1,0:T(1,128)S(1)}, u32[]{:S(2)}, u32[]{:S(2)}) %all-to-all-start.4) | async-done | bytes 20512 | tf_op jit(solution)/shard_map/all_to_all | solution.py:158
  101.4 0.6 copy.25
  102.0 2.3 %to_second.1 = (f32[1,640]{1,0:T(1,128)}, f32[8,1280]{1,0:T(8,128)}) custom-call(f32[8,640]{1,0:T(8,128)} %bitcast.29, f32[1,1152]{1,0:T(1,128)} %get-tuple-element.23.proj_ref, f32[1,512]{1,0:T(1,128)} %get-tuple-element.24.grad_ref, f32[1,128]{1,0:T(1,128)} %get-tuple-element.25.count_ref, bf16[1024,512]{1,0:T(8,128)(2,1)} %get-tuple-element.18.rows_ref), custom_call_target="tpu_custom_call" | custom-call | tf_op jit(solution)/shard_map/to_second/pallas_call | solution.py:34
  104.3 1.4 %copy.10 = f32[8,1,1280]{2,1,0:T(1,128)} copy(f32[8,1,1280]{2,0,1:T(8,128)} %bitcast.31) | data formatting | bytes 81920 | tf_op jit(solution)/shard_map/all_to_all | solution.py:158
  105.8 5.1 %all-to-all-start.5 = ((f32[8,1,1280]{2,1,0:T(1,128)}), f32[8,1,1280]{2,1,0:T(1,128)S(1)}, u32[]{:S(2)}, u32[]{:S(2)}) async-start(f32[8,1,1280]{2,1,0:T(1,128)} %copy.10), calls=%async_computation.5 | async-start | bytes 81920 | tf_op jit(solution)/shard_map/all_to_all | solution.py:158
  110.9 1.2 constant_dynamic-slice_fusion.1.grad_ref
  112.1 3.6 %all-to-all-done.5 = f32[8,1,1280]{2,1,0:T(1,128)S(1)} async-done(((f32[8,1,1280]{2,1,0:T(1,128)}), f32[8,1,1280]{2,1,0:T(1,128)S(1)}, u32[]{:S(2)}, u32[]{:S(2)}) %all-to-all-start.5) | async-done | bytes 40992 | tf_op jit(solution)/shard_map/all_to_all | solution.py:158
  115.7 0.6 copy.22
  116.3 1.6 %to_bend.1 = (f32[8,128]{1,0:T(8,128)}, f32[8,128]{1,0:T(8,128)}) custom-call(f32[8,1280]{1,0:T(8,128)} %bitcast.26, f32[1,1152]{1,0:T(1,128)} %get-tuple-element.23.proj_ref, f32[8,1024]{1,0:T(8,128)} %get-tuple-element.21.curv_ref), custom_call_target="tpu_custom_call" | custom-call | tf_op jit(solution)/shard_map/to_bend/pallas_call | solution.py:34
  117.9 3.3 %all-to-all-start.6 = ((f32[8,1,128]{2,1,0:T(1,128)}), f32[8,1,128]{2,1,0:T(1,128)S(1)}, u32[]{:S(2)}, u32[]{:S(2)}) async-start(f32[8,1,128]{2,1,0:T(1,128)} %bitcast.37), calls=%async_computation.6 | async-start | bytes 8192 | tf_op jit(solution)/shard_map/all_to_all | solution.py:158
  121.1 1.2 constant_dynamic-slice_fusion.resid_ref
  122.3 1.2 slice.3.first_ref
  123.6 4.0 %all-to-all-done.6 = f32[8,1,128]{2,1,0:T(1,128)S(1)} async-done(((f32[8,1,128]{2,1,0:T(1,128)}), f32[8,1,128]{2,1,0:T(1,128)S(1)}, u32[]{:S(2)}, u32[]{:S(2)}) %all-to-all-start.6) | async-done | bytes 4128 | tf_op jit(solution)/shard_map/all_to_all | solution.py:158
  127.6 0.0 copy-start
  127.6 0.6 copy-done
  128.2 1.3 to_step.1
Async XLA Ops:
  91.5 9.9 %all-to-all-start.4 = ((f32[8,1,640]{2,1,0:T(1,128)}), f32[8,1,640]{2,1,0:T(1,128)S(1)}, u32[]{:S(2)}, u32[]{:S(2)}) async-start(f32[8,1,640]{2,1,0:T(1,128)} %copy.9), calls=%async_computation.4 | async-start | bytes 40960 | tf_op jit(solution)/shard_map/all_to_all | solution.py:158
  105.8 9.9 %all-to-all-start.5 = ((f32[8,1,1280]{2,1,0:T(1,128)}), f32[8,1,1280]{2,1,0:T(1,128)S(1)}, u32[]{:S(2)}, u32[]{:S(2)}) async-start(f32[8,1,1280]{2,1,0:T(1,128)} %copy.10), calls=%async_computation.5 | async-start | bytes 81920 | tf_op jit(solution)/shard_map/all_to_all | solution.py:158
  117.9 9.7 %all-to-all-start.6 = ((f32[8,1,128]{2,1,0:T(1,128)}), f32[8,1,128]{2,1,0:T(1,128)S(1)}, u32[]{:S(2)}, u32[]{:S(2)}) async-start(f32[8,1,128]{2,1,0:T(1,128)} %bitcast.37), calls=%async_computation.6 | async-start | bytes 8192 | tf_op jit(solution)/shard_map/all_to_all | solution.py:158
  127.6 0.6 copy-start

commit v2 on v1

v2 whole, which is shorter than its diff:
```python
import functools

import jax
import jax.numpy as jnp
from jax import lax
from jax.experimental import pallas as pl
from jax.experimental.pallas import tpu as pltpu
from jax.sharding import PartitionSpec as P

penalty = 0.1
PEERS = 8
LANES = 128
GRANT = 12 << 20
f32 = jnp.float32
bf16 = jnp.bfloat16


def nt(a, b):
    return lax.dot_general(a, b, (((1,), (1,)), ((), ())), preferred_element_type=f32)


def nn(a, b):
    return lax.dot_general(a, b, (((1,), (0,)), ((), ())), preferred_element_type=f32)


def rep(row):
    return jnp.broadcast_to(row, (PEERS, row.shape[1]))


def total_of(ref):
    parts = [ref[p] for p in range(PEERS)]
    while len(parts) > 1:
        parts = [a + b for a, b in zip(parts[::2], parts[1::2])]
    return parts[0]


def send(ref, *rows):
    at = 0
    for row in rows:
        for p in range(PEERS):
            ref[p, :, at : at + row.shape[1]] = row
        at = at + row.shape[1]


def lanes(scalar):
    return jnp.broadcast_to(scalar, (1, LANES))


def row_sum(row):
    return jnp.sum(row, axis=1, keepdims=True)


def call(kernel, *args, out):
    return pl.pallas_call(
        kernel,
        out_shape=out,
        in_specs=[pl.BlockSpec(memory_space=pltpu.VMEM)] * len(args),
        out_specs=jax.tree.map(lambda _: pl.BlockSpec(memory_space=pltpu.VMEM), out),
        compiler_params=pltpu.CompilerParams(vmem_limit_bytes=GRANT),
        name=kernel.func.__name__ if isinstance(kernel, functools.partial) else kernel.__name__,
    )(*args)


def shape(*dims, dtype=f32):
    return jax.ShapeDtypeStruct(dims, dtype)


def pack_rows(cap, ids_ref, lab_ref, emb_ref, out_ref):
    rows = emb_ref.shape[0]
    ids = ids_ref[...]
    heads = lax.broadcasted_iota(jnp.int32, (PEERS, rows), 0)
    members = heads == ids
    mem_f = members.astype(f32)
    earlier = lax.broadcasted_iota(jnp.int32, (rows, rows), 0) < lax.broadcasted_iota(
        jnp.int32, (rows, rows), 1
    )
    before = nn(mem_f.astype(bf16), earlier.astype(f32).astype(bf16))
    rank = jnp.sum(before * mem_f, axis=0, keepdims=True).astype(jnp.int32)
    at_rank = lax.broadcasted_iota(jnp.int32, (cap, rows), 0) == rank
    tags = (lab_ref[...] + 1).astype(f32)
    tag_slots = nt((mem_f * tags).astype(bf16), at_rank.astype(f32).astype(bf16))
    emb = emb_ref[...]
    for p in range(PEERS):
        pick = (at_rank & (ids == p)).astype(f32).astype(bf16)
        out_ref[p, :cap, :] = nn(pick, emb).astype(bf16)
        out_ref[p, cap:, :cap] = jnp.broadcast_to(tag_slots[p : p + 1], (PEERS, cap)).astype(bf16)
        out_ref[p, cap:, cap:] = jnp.zeros((PEERS, rows - cap), bf16)


def take_rows(cap, got_ref, w_ref, rows_ref, tags_ref, out_ref):
    for p in range(PEERS):
        rows_ref[p * cap : (p + 1) * cap, :] = got_ref[p, :cap, :]
        tags_ref[:, p * cap : (p + 1) * cap] = got_ref[p, cap:, :cap].astype(f32)[:1]
    send(out_ref, nt(rep(w_ref[...]).astype(bf16), rows_ref[...])[:1])


def to_residual(got_ref, tags_ref, rows_ref, curv_ref, out_ref):
    logits = total_of(got_ref)
    tags = tags_ref[...]
    valid = tags > 0.0
    prob = jax.nn.sigmoid(logits)
    residual = jnp.where(valid, prob - jnp.maximum(tags - 1.0, 0.0), 0.0)
    curv_ref[...] = jnp.where(valid, prob * (1.0 - prob), 0.0)
    part = nn(rep(residual).astype(bf16), rows_ref[...])[:1]
    send(out_ref, part, lanes(row_sum(valid.astype(f32))))


def to_direction(got_ref, w_ref, rows_ref, grad_ref, count_ref, out_ref):
    width = rows_ref.shape[1]
    total = total_of(got_ref)
    count = total[:, width : width + 1]
    grad = total[:, :width] / count + penalty * w_ref[...]
    grad_ref[...] = grad
    count_ref[...] = lanes(count)
    part = nt(rep(-grad).astype(bf16), rows_ref[...])[:1]
    send(out_ref, part, lanes(row_sum(grad * grad)))


def to_image(got_ref, curv_ref, rows_ref, proj_ref, out_ref):
    slots = rows_ref.shape[0]
    total = total_of(got_ref)
    proj_ref[...] = total
    proj = total[:, :slots]
    weighted = (curv_ref[...] * proj).astype(bf16).astype(f32)
    part = nn(rep(weighted).astype(bf16), rows_ref[...])[:1]
    send(out_ref, part, lanes(row_sum(weighted * proj)))


def to_second(got_ref, proj_ref, grad_ref, count_ref, rows_ref, resid_ref, step_ref, out_ref):
    width, slots = rows_ref.shape[1], rows_ref.shape[0]
    total = total_of(got_ref)
    count = count_ref[:, :1]
    sq_norm = proj_ref[:, slots : slots + 1]
    direction = -grad_ref[...]
    image = total[:, :width] / count + penalty * direction
    step = sq_norm / (total[:, width : width + 1] / count + penalty * sq_norm)
    resid = direction - step * image
    resid_ref[...] = resid
    step_ref[...] = lanes(step)
    part = nt(rep(resid).astype(bf16), rows_ref[...])[:1]
    send(out_ref, part, lanes(row_sum(resid * resid)), lanes(row_sum(resid * direction)))


def to_bend(got_ref, proj_ref, curv_ref, keep_ref, out_ref):
    slots = curv_ref.shape[1]
    total = total_of(got_ref)
    sq_norm = proj_ref[:, slots : slots + 1]
    sq_next = total[:, slots : slots + 1]
    cross = total[:, slots + LANES : slots + LANES + 1]
    beta = sq_next / sq_norm
    proj = total[:, :slots] + beta * proj_ref[:, :slots]
    weighted = (curv_ref[...] * proj).astype(bf16).astype(f32)
    send(out_ref, lanes(row_sum(weighted * proj)))
    dir_sq = sq_next + 2.0 * beta * cross + beta * beta * sq_norm
    keep_ref[:, :LANES] = lanes(beta)
    keep_ref[:, LANES : 2 * LANES] = lanes(sq_next)
    keep_ref[:, 2 * LANES :] = lanes(dir_sq)


def to_step(got_ref, count_ref, keep_ref, first_ref, grad_ref, resid_ref, out_ref):
    beta = keep_ref[:, :1]
    sq_next = keep_ref[:, LANES : LANES + 1]
    dir_sq = keep_ref[:, 2 * LANES : 2 * LANES + 1]
    bend = total_of(got_ref)[:, :1]
    step = sq_next / (bend / count_ref[:, :1] + penalty * dir_sq)
    direction = -grad_ref[...]
    out_ref[...] = first_ref[:, :1] * direction + step * (resid_ref[...] + beta * direction)


def exchange(values, axis):
    return lax.all_to_all(values, axis, split_axis=0, concat_axis=0, tiled=True)


def shards(embeddings, plant_ids, labels, weights):
    rows_here, width = embeddings.shape
    samps = lax.axis_size("samp")
    share = width // samps
    cap = 2 * rows_here // PEERS
    slots = PEERS * cap
    at = lax.axis_index("samp") * share

    sent = call(
        functools.partial(pack_rows, cap),
        plant_ids.reshape(1, rows_here),
        labels.reshape(1, rows_here),
        embeddings,
        out=shape(PEERS, cap + PEERS, width, dtype=bf16),
    )
    got = exchange(sent, "plant")
    rows, tags, part = call(
        functools.partial(take_rows, cap),
        got,
        weights,
        out=(shape(slots, width, dtype=bf16), shape(1, slots), shape(PEERS, 1, slots)),
    )
    got = exchange(part, "feat")
    curv, part = call(
        to_residual, got, tags, rows, out=(shape(1, slots), shape(PEERS, 1, width + LANES))
    )
    got = exchange(part, "samp")
    grad, count, part = call(
        to_direction,
        got,
        weights,
        rows,
        out=(shape(1, width), shape(1, LANES), shape(PEERS, 1, slots + LANES)),
    )
    got = exchange(part, "feat")
    proj, part = call(
        to_image, got, curv, rows, out=(shape(1, slots + LANES), shape(PEERS, 1, width + LANES))
    )
    got = exchange(part, "samp")
    resid, first, part = call(
        to_second,
        got,
        proj,
        grad,
        count,
        rows,
        out=(shape(1, width), shape(1, LANES), shape(PEERS, 1, slots + 2 * LANES)),
    )
    got = exchange(part, "feat")
    scalars, part = call(
        to_bend, got, proj, curv, out=(shape(1, 3 * LANES), shape(PEERS, 1, LANES))
    )
    got = exchange(part, "samp")
    grad_share = lax.dynamic_slice_in_dim(grad, at, share, 1)
    resid_share = lax.dynamic_slice_in_dim(resid, at, share, 1)
    newton_step = call(
        to_step,
        got,
        count,
        scalars,
        first,
        grad_share,
        resid_share,
        out=shape(1, share),
    )
    return newton_step, grad_share


def solution(mesh):
    placed = (
        P(("plant", "samp"), "feat"),
        P(("plant", "samp"), None),
        P(("plant", "samp")),
        P("plant", "feat"),
    )
    return jax.shard_map(
        shards,
        mesh=mesh,
        in_specs=placed,
        out_specs=(P("plant", ("feat", "samp")), P("plant", ("feat", "samp"))),
        check_vma=False,
    )
```

time: 130 us -> 111 us (0.85)
  Pallas kernels: 17.1 us -> 5.18 us
  local copies, waits for them, and re-layouts: 12.4 us -> 2.56 us
  waiting for transfers between devices: 14.1 us -> 17.6 us
    pallas_call x8, Pallas kernels: 17.1 us -> 5.18 us  [call(): pl.pallas_call(kernel, out_shape=out, in_specs=[pl.BlockSpec(memory_space...]
    all_to_all x5 -> x0, local copies, waits for them, and re-layouts: 5.12 us -> none  [exchange(): return lax.all_to_all(values, axis, split_axis=0, concat_axis=0, tiled=True)]
    all_to_all x3, waiting for transfers between devices: 14.1 us -> 17.6 us  [exchange(): return lax.all_to_all(values, axis, split_axis=0, concat_axis=0, tiled=True)]
    unnamed x7 -> x10, local copies, waits for them, and re-layouts: 3.64 us -> 2.41 us
  transfers between devices with their start and end apart: 3 -> 3, of which waited for: 3 -> 3; matrix products, arithmetic and copies ran while one was open for 3% -> 0% of each run, Pallas kernels for 0% -> 0%
where the time goes in v2:
time: 111 us
  blocking collectives  73.1 us (66%)
  waiting for transfers between devices  17.6 us (16%)
  starting transfers between devices  11.7 us (11%)
  Pallas kernels  5.18 us (5%)
  local copies, waits for them, and re-layouts  2.56 us (2%)
    all_to_all x4, blocking collectives, exchange(): return lax.all_to_all(values, axis, split_axis=0, concat_axis=0, tiled=True)  73.1 us
    all_to_all x3, waiting for transfers between devices, exchange(): return lax.all_to_all(values, axis, split_axis=0, concat_axis=0, tiled=True)  17.6 us
    all_to_all x3, starting transfers between devices, exchange(): return lax.all_to_all(values, axis, split_axis=0, concat_axis=0, tiled=True)  11.7 us
    pallas_call x8, Pallas kernels, call(): pl.pallas_call(kernel, out_shape=out, in_specs=[pl.BlockSpec(memory_space...  5.18 us
    unnamed x10, local copies, waits for them, and re-layouts  2.41 us
  transfers between devices with their start and end apart: 3, of which 3 were waited for; matrix products, arithmetic and copies ran while one was open for 0% of the time, Pallas kernels for 0%

profile of v2, /device:TPU:1, one launch (start us, length us, event | category | flops | bytes accessed | tf_op | source)
XLA Modules:
  0.0 110.9 jit_solution(6558615733089795936)
XLA Ops:
  0.6 0.0 copy-start
  0.6 1.0 copy-done
  1.7 0.0 copy-start.2
  1.7 0.7 copy-done.2
  2.4 0.0 copy-start.3
  2.4 0.7 copy-done.3
  3.0 0.9 pack_rows.1
  4.0 0.0 copy-start.1
  4.0 39.4 %all_to_all.35.got_ref = bf16[8,136,512]{2,1,0:T(8,128)(2,1)S(1)} all-to-all(bf16[8,136,512]{2,1,0:T(8,128)(2,1)S(1)} %pack_rows.1), channel_id=1, replica_groups=mesh['plant'=8,'feat'=8,'samp'=8] {'plant'}, dimensions={0} | all-to-all | bytes 2228224 | tf_op jit(solution)/shard_map/all_to_all | solution.py:171
  43.3 0.0 copy-done.1
  43.3 0.4 take_rows.1
  43.7 11.2 %all_to_all.36.got_ref = f32[8,1,1024]{2,1,0:T(1,128)S(1)} all-to-all(f32[8,1,1024]{2,1,0:T(1,128)S(1)} %get-tuple-element.17), channel_id=1, replica_groups=mesh['plant'=8,'feat'=8,'samp'=8] {'feat'}, dimensions={0} | all-to-all | bytes 65536 | tf_op jit(solution)/shard_map/all_to_all | solution.py:171
  54.9 0.2 to_residual.1
  55.2 13.3 %all_to_all.37.got_ref = f32[8,1,640]{2,1,0:T(1,128)S(1)} all-to-all(f32[8,1,640]{2,1,0:T(1,128)S(1)} %get-tuple-element.20), channel_id=1, replica_groups=mesh['plant'=8,'feat'=8,'samp'=8] {'samp'}, dimensions={0} | all-to-all | bytes 40960 | tf_op jit(solution)/shard_map/all_to_all | solution.py:171
  68.5 0.4 to_direction.1
  68.8 9.3 %all_to_all.38.got_ref = f32[8,1,1152]{2,1,0:T(1,128)S(1)} all-to-all(f32[8,1,1152]{2,1,0:T(1,128)S(1)} %get-tuple-element.21), channel_id=1, replica_groups=mesh['plant'=8,'feat'=8,'samp'=8] {'feat'}, dimensions={0} | all-to-all | bytes 73728 | tf_op jit(solution)/shard_map/all_to_all | solution.py:171
  78.1 0.9 to_image.1
  79.0 3.3 %all-to-all-start.4 = ((f32[8,1,640]{2,1,0:T(1,128)}), f32[8,1,640]{2,1,0:T(1,128)S(1)}, u32[]{:S(2)}, u32[]{:S(2)}) async-start(f32[8,1,640]{2,1,0:T(1,128)} %get-tuple-element.23), calls=%async_computation.4 | async-start | bytes 40960 | tf_op jit(solution)/shard_map/all_to_all | solution.py:171
  82.3 6.6 %all-to-all-done.4.got_ref = f32[8,1,640]{2,1,0:T(1,128)S(1)} async-done(((f32[8,1,640]{2,1,0:T(1,128)}), f32[8,1,640]{2,1,0:T(1,128)S(1)}, u32[]{:S(2)}, u32[]{:S(2)}) %all-to-all-start.4) | async-done | bytes 20512 | tf_op jit(solution)/shard_map/all_to_all | solution.py:171
  88.9 1.0 to_second.1
  89.9 5.1 %all-to-all-start.5 = ((f32[8,1,1280]{2,1,0:T(1,128)}), f32[8,1,1280]{2,1,0:T(1,128)S(1)}, u32[]{:S(2)}, u32[]{:S(2)}) async-start(f32[8,1,1280]{2,1,0:T(1,128)} %get-tuple-element.27), calls=%async_computation.5 | async-start | bytes 81920 | tf_op jit(solution)/shard_map/all_to_all | solution.py:171
  95.0 0.1 constant_dynamic-slice_fusion.1.grad_ref
  95.1 0.0 copy-start.4
  95.1 4.7 %all-to-all-done.5.got_ref = f32[8,1,1280]{2,1,0:T(1,128)S(1)} async-done(((f32[8,1,1280]{2,1,0:T(1,128)}), f32[8,1,1280]{2,1,0:T(1,128)S(1)}, u32[]{:S(2)}, u32[]{:S(2)}) %all-to-all-start.5) | async-done | bytes 40992 | tf_op jit(solution)/shard_map/all_to_all | solution.py:171
  99.8 0.8 to_bend.1
  100.6 3.3 %all-to-all-start.6 = ((f32[8,1,128]{2,1,0:T(1,128)}), f32[8,1,128]{2,1,0:T(1,128)S(1)}, u32[]{:S(2)}, u32[]{:S(2)}) async-start(f32[8,1,128]{2,1,0:T(1,128)} %get-tuple-element.28), calls=%async_computation.6 | async-start | bytes 8192 | tf_op jit(solution)/shard_map/all_to_all | solution.py:171
  103.8 0.1 constant_dynamic-slice_fusion.resid_ref
  103.9 6.4 %all-to-all-done.6.got_ref = f32[8,1,128]{2,1,0:T(1,128)S(1)} async-done(((f32[8,1,128]{2,1,0:T(1,128)}), f32[8,1,128]{2,1,0:T(1,128)S(1)}, u32[]{:S(2)}, u32[]{:S(2)}) %all-to-all-start.6) | async-done | bytes 4128 | tf_op jit(solution)/shard_map/all_to_all | solution.py:171
  110.3 0.6 to_step.1
  110.9 0.0 copy-done.4
Async XLA Ops:
  0.6 1.0 copy-start
  1.7 0.7 copy-start.2
  2.4 0.7 copy-start.3
  4.0 39.4 %copy-start.1 = (f32[1,512]{1,0:T(1,128)S(1)}, f32[1,512]{1,0:T(1,128)}, u32[]{:S(2)}) copy-start(f32[1,512]{1,0:T(1,128)} %w_ref.3) | copy-start | bytes 6148
  79.0 9.9 %all-to-all-start.4 = ((f32[8,1,640]{2,1,0:T(1,128)}), f32[8,1,640]{2,1,0:T(1,128)S(1)}, u32[]{:S(2)}, u32[]{:S(2)}) async-start(f32[8,1,640]{2,1,0:T(1,128)} %get-tuple-element.23), calls=%async_computation.4 | async-start | bytes 40960 | tf_op jit(solution)/shard_map/all_to_all | solution.py:171
  89.9 9.9 %all-to-all-start.5 = ((f32[8,1,1280]{2,1,0:T(1,128)}), f32[8,1,1280]{2,1,0:T(1,128)S(1)}, u32[]{:S(2)}, u32[]{:S(2)}) async-start(f32[8,1,1280]{2,1,0:T(1,128)} %get-tuple-element.27), calls=%async_computation.5 | async-start | bytes 81920 | tf_op jit(solution)/shard_map/all_to_all | solution.py:171
  95.1 15.8 %copy-start.4 = (f32[1,64]{1,0:T(1,128)}, f32[1,64]{1,0:T(1,128)S(1)}, u32[]{:S(2)}) copy-start(f32[1,64]{1,0:T(1,128)S(1)} %constant_dynamic-slice_fusion.1.grad_ref) | copy-start | bytes 772
  100.6 9.7 %all-to-all-start.6 = ((f32[8,1,128]{2,1,0:T(1,128)}), f32[8,1,128]{2,1,0:T(1,128)S(1)}, u32[]{:S(2)}, u32[]{:S(2)}) async-start(f32[8,1,128]{2,1,0:T(1,128)} %get-tuple-element.28), calls=%async_computation.6 | async-start | bytes 8192 | tf_op jit(solution)/shard_map/all_to_all | solution.py:171

commit v3 on v2

--- a/solution.py
+++ b/solution.py
@@ -50,11 +50,12 @@
     return jnp.sum(row, axis=1, keepdims=True)
 
 
-def call(kernel, *args, out):
+def call(kernel, *args, out, scratch=(), space=pltpu.VMEM):
     return pl.pallas_call(
         kernel,
         out_shape=out,
-        in_specs=[pl.BlockSpec(memory_space=pltpu.VMEM)] * len(args),
+        in_specs=[pl.BlockSpec(memory_space=space)] * len(args),
+        scratch_shapes=scratch,
         out_specs=jax.tree.map(lambda _: pl.BlockSpec(memory_space=pltpu.VMEM), out),
         compiler_params=pltpu.CompilerParams(vmem_limit_bytes=GRANT),
         name=kernel.func.__name__ if isinstance(kernel, functools.partial) else kernel.__name__,
@@ -65,20 +66,31 @@
     return jax.ShapeDtypeStruct(dims, dtype)
 
 
-def pack_rows(cap, ids_ref, lab_ref, emb_ref, out_ref):
+def pack_rows(cap, ids_in, lab_in, emb_in, out_ref, ids_ref, lab_ref, emb_ref, sems):
+    copies = [
+        pltpu.make_async_copy(src, dst, sems.at[k])
+        for k, (src, dst) in enumerate(
+            ((ids_in, ids_ref), (lab_in, lab_ref), (emb_in, emb_ref))
+        )
+    ]
+    for copy in copies:
+        copy.start()
     rows = emb_ref.shape[0]
-    ids = ids_ref[...]
     heads = lax.broadcasted_iota(jnp.int32, (PEERS, rows), 0)
-    members = heads == ids
-    mem_f = members.astype(f32)
     earlier = lax.broadcasted_iota(jnp.int32, (rows, rows), 0) < lax.broadcasted_iota(
         jnp.int32, (rows, rows), 1
     )
-    before = nn(mem_f.astype(bf16), earlier.astype(f32).astype(bf16))
+    earlier = earlier.astype(f32).astype(bf16)
+    copies[0].wait()
+    copies[1].wait()
+    ids = ids_ref[...]
+    mem_f = (heads == ids).astype(f32)
+    before = nn(mem_f.astype(bf16), earlier)
     rank = jnp.sum(before * mem_f, axis=0, keepdims=True).astype(jnp.int32)
     at_rank = lax.broadcasted_iota(jnp.int32, (cap, rows), 0) == rank
     tags = (lab_ref[...] + 1).astype(f32)
     tag_slots = nt((mem_f * tags).astype(bf16), at_rank.astype(f32).astype(bf16))
+    copies[2].wait()
     emb = emb_ref[...]
     for p in range(PEERS):
         pick = (at_rank & (ids == p)).astype(f32).astype(bf16)
@@ -116,55 +128,70 @@
     send(out_ref, part, lanes(row_sum(grad * grad)))
 
 
-def to_image(got_ref, curv_ref, rows_ref, proj_ref, out_ref):
+def to_image(got_ref, curv_ref, rows_ref, sq_norm_ref, out_ref):
     slots = rows_ref.shape[0]
     total = total_of(got_ref)
-    proj_ref[...] = total
+    sq_norm_ref[...] = total[:, slots:]
     proj = total[:, :slots]
-    weighted = (curv_ref[...] * proj).astype(bf16).astype(f32)
+    curv = curv_ref[...]
+    weighted = (curv * proj).astype(bf16).astype(f32)
     part = nn(rep(weighted).astype(bf16), rows_ref[...])[:1]
-    send(out_ref, part, lanes(row_sum(weighted * proj)))
-
-
-def to_second(got_ref, proj_ref, grad_ref, count_ref, rows_ref, resid_ref, step_ref, out_ref):
-    width, slots = rows_ref.shape[1], rows_ref.shape[0]
-    total = total_of(got_ref)
+    send(out_ref, part, lanes(row_sum(weighted * proj)), jnp.sqrt(curv) * proj)
+
+
+def to_second(got_ref, sq_norm_ref, curv_ref, grad_ref, count_ref, rows_ref, resid_ref, step_ref, out_ref):
+    width, cap = rows_ref.shape[1], rows_ref.shape[0] // PEERS
+    total = got_ref[0, :, : width + LANES]
+    for p in range(1, PEERS):
+        total = total + got_ref[p, :, : width + LANES]
     count = count_ref[:, :1]
-    sq_norm = proj_ref[:, slots : slots + 1]
+    sq_norm = sq_norm_ref[:, :1]
     direction = -grad_ref[...]
     image = total[:, :width] / count + penalty * direction
     step = sq_norm / (total[:, width : width + 1] / count + penalty * sq_norm)
     resid = direction - step * image
     resid_ref[...] = resid
     step_ref[...] = lanes(step)
-    part = nt(rep(resid).astype(bf16), rows_ref[...])[:1]
-    send(out_ref, part, lanes(row_sum(resid * resid)), lanes(row_sum(resid * direction)))
-
-
-def to_bend(got_ref, proj_ref, curv_ref, keep_ref, out_ref):
-    slots = curv_ref.shape[1]
-    total = total_of(got_ref)
-    sq_norm = proj_ref[:, slots : slots + 1]
-    sq_next = total[:, slots : slots + 1]
-    cross = total[:, slots + LANES : slots + LANES + 1]
+    part = nt(rep(resid).astype(bf16), rows_ref[...]) * jnp.sqrt(curv_ref[...])
+    source = lax.broadcasted_iota(jnp.int32, (PEERS, cap), 0)
+    tile = part[:, :cap]
+    for p in range(1, PEERS):
+        tile = jnp.where(source == p, part[:, p * cap : (p + 1) * cap], tile)
+    tile = tile.astype(bf16)
+    for peer in range(out_ref.shape[0]):
+        out_ref[peer] = tile
+
+
+def to_tiles(got_ref, out_ref):
+    groups, cap = out_ref.shape[0], out_ref.shape[2]
+    start = got_ref.shape[2] - PEERS * cap
+    for s in range(groups):
+        for p in range(PEERS):
+            out_ref[s, p : p + 1, :] = got_ref[s, :, start + p * cap : start + (p + 1) * cap]
+
+
+def to_step(got_ref, first_ref, count_ref, sq_norm_ref, step_ref, grad_ref, resid_ref, out_ref):
+    groups = first_ref.shape[0]
+    feats = got_ref.shape[0] // groups
+    first_sq, cross, second_sq = 0.0, 0.0, 0.0
+    for s in range(groups):
+        first = first_ref[s]
+        second = got_ref[s].astype(f32)
+        for f in range(1, feats):
+            second = second + got_ref[f * groups + s].astype(f32)
+        first_sq = first_sq + first * first
+        cross = cross + first * second
+        second_sq = second_sq + second * second
+    first_sq, cross, second_sq = (
+        jnp.sum(row_sum(v), axis=0, keepdims=True) for v in (first_sq, cross, second_sq)
+    )
+    count, sq_norm, first_step = count_ref[:, :1], sq_norm_ref[:, :1], step_ref[:, :1]
+    sq_next = -first_step * cross / count
     beta = sq_next / sq_norm
-    proj = total[:, :slots] + beta * proj_ref[:, :slots]
-    weighted = (curv_ref[...] * proj).astype(bf16).astype(f32)
-    send(out_ref, lanes(row_sum(weighted * proj)))
-    dir_sq = sq_next + 2.0 * beta * cross + beta * beta * sq_norm
-    keep_ref[:, :LANES] = lanes(beta)
-    keep_ref[:, LANES : 2 * LANES] = lanes(sq_next)
-    keep_ref[:, 2 * LANES :] = lanes(dir_sq)
-
-
-def to_step(got_ref, count_ref, keep_ref, first_ref, grad_ref, resid_ref, out_ref):
-    beta = keep_ref[:, :1]
-    sq_next = keep_ref[:, LANES : LANES + 1]
-    dir_sq = keep_ref[:, 2 * LANES : 2 * LANES + 1]
-    bend = total_of(got_ref)[:, :1]
-    step = sq_next / (bend / count_ref[:, :1] + penalty * dir_sq)
+    bend = second_sq + 2.0 * beta * cross + beta * beta * first_sq
+    step = sq_next / (bend / count + penalty * (sq_next + beta * beta * sq_norm))
     direction = -grad_ref[...]
-    out_ref[...] = first_ref[:, :1] * direction + step * (resid_ref[...] + beta * direction)
+    out_ref[...] = first_step * direction + step * (resid_ref[...] + beta * direction)
 
 
 def exchange(values, axis):
@@ -181,10 +208,18 @@
 
     sent = call(
         functools.partial(pack_rows, cap),
-        plant_ids.reshape(1, rows_here),
-        labels.reshape(1, rows_here),
-        embeddings,
+        *(
+            pltpu.with_memory_space_constraint(v, pltpu.HBM)
+            for v in (plant_ids.reshape(1, rows_here), labels.reshape(1, rows_here), embeddings)
+        ),
         out=shape(PEERS, cap + PEERS, width, dtype=bf16),
+        scratch=(
+            pltpu.VMEM((1, rows_here), jnp.int32),
+            pltpu.VMEM((1, rows_here), jnp.int32),
+            pltpu.VMEM((rows_here, width), bf16),
+            pltpu.SemaphoreType.DMA((3,)),
+        ),
+        space=pltpu.HBM,
     )
     got = exchange(sent, "plant")
     rows, tags, part = call(
@@ -206,32 +241,39 @@
         out=(shape(1, width), shape(1, LANES), shape(PEERS, 1, slots + LANES)),
     )
     got = exchange(part, "feat")
-    proj, part = call(
-        to_image, got, curv, rows, out=(shape(1, slots + LANES), shape(PEERS, 1, width + LANES))
+    sq_norm, part = call(
+        to_image,
+        got,
+        curv,
+        rows,
+        out=(shape(1, LANES), shape(PEERS, 1, width + LANES + slots)),
     )
     got = exchange(part, "samp")
-    resid, first, part = call(
+    resid, first_step, part = call(
         to_second,
         got,
-        proj,
+        sq_norm,
+        curv,
         grad,
         count,
         rows,
-        out=(shape(1, width), shape(1, LANES), shape(PEERS, 1, slots + 2 * LANES)),
-    )
-    got = exchange(part, "feat")
-    scalars, part = call(
-        to_bend, got, proj, curv, out=(shape(1, 3 * LANES), shape(PEERS, 1, LANES))
-    )
-    got = exchange(part, "samp")
+        out=(
+            shape(1, width),
+            shape(1, LANES),
+            shape(lax.axis_size("feat") * samps, PEERS, cap, dtype=bf16),
+        ),
+    )
+    first = call(to_tiles, got, out=shape(samps, PEERS, cap))
+    got = exchange(part, ("feat", "samp"))
     grad_share = lax.dynamic_slice_in_dim(grad, at, share, 1)
     resid_share = lax.dynamic_slice_in_dim(resid, at, share, 1)
     newton_step = call(
         to_step,
         got,
+        first,
         count,
-        scalars,
-        first,
+        sq_norm,
+        first_step,
         grad_share,
         resid_share,
         out=shape(1, share),

time: 111 us -> 105 us (0.946)
  blocking collectives: 73.1 us -> 82.6 us
  waiting for transfers between devices: 17.6 us -> 9.86 us
  starting transfers between devices: 11.7 us -> 5.91 us
  local copies, waits for them, and re-layouts: 2.56 us -> 0.16 us
    all_to_all x4 -> x5, blocking collectives: 73.1 us -> 82.6 us  [exchange(): return lax.all_to_all(values, axis, split_axis=0, concat_axis=0, tiled=True)]
    all_to_all x3 -> x1, waiting for transfers between devices: 17.6 us -> 9.86 us  [exchange(): return lax.all_to_all(values, axis, split_axis=0, concat_axis=0, tiled=True)]
    all_to_all x3 -> x1, starting transfers between devices: 11.7 us -> 5.91 us  [exchange(): return lax.all_to_all(values, axis, split_axis=0, concat_axis=0, tiled=True)]
    unnamed x10 -> x4, local copies, waits for them, and re-layouts: 2.41 us -> 0.01 us
  transfers between devices with their start and end apart: 3 -> 1, of which waited for: 3 -> 1; matrix products, arithmetic and copies ran while one was open for 0% -> 0% of each run, Pallas kernels for 0% -> 0%
where the time goes in v3:
time: 105 us; the launch traced here: 104 us
  blocking collectives  82.6 us (79%)
  waiting for transfers between devices  9.86 us (9%)
  starting transfers between devices  5.91 us (6%)
  Pallas kernels  4.9 us (5%)
    all_to_all x5, blocking collectives, exchange(): return lax.all_to_all(values, axis, split_axis=0, concat_axis=0, tiled=True)  82.6 us
    all_to_all x1, waiting for transfers between devices, exchange(): return lax.all_to_all(values, axis, split_axis=0, concat_axis=0, tiled=True)  9.86 us
    all_to_all x1, starting transfers between devices, exchange(): return lax.all_to_all(values, axis, split_axis=0, concat_axis=0, tiled=True)  5.91 us
    pallas_call x8, Pallas kernels, call(): pl.pallas_call(kernel, out_shape=out, in_specs=[pl.BlockSpec(memory_space...  4.9 us
  transfers between devices with their start and end apart: 1, of which 1 were waited for; matrix products, arithmetic and copies ran while one was open for 0% of the time, Pallas kernels for 0%

profile of v3, /device:TPU:1, one launch (start us, length us, event | category | flops | bytes accessed | tf_op | source)
XLA Modules:
  0.0 104.1 jit_solution(9896643942465692110)
XLA Ops:
  0.6 1.8 %pack_rows.1 = bf16[8,136,512]{2,1,0:T(8,128)(2,1)S(1)} custom-call(s32[1,512]{1,0:T(1,128)} %bitcast.2, s32[1,512]{1,0:T(1,128)} %bitcast.3, bf16[512,512]{1,0:T(8,128)(2,1)} %emb_in.1), custom_call_target="tpu_custom_call" | custom-call | tf_op jit(solution)/shard_map/pack_rows/pallas_call | solution.py:54
  2.5 0.0 copy-start
  2.5 39.3 %all_to_all.30.got_ref = bf16[8,136,512]{2,1,0:T(8,128)(2,1)S(1)} all-to-all(bf16[8,136,512]{2,1,0:T(8,128)(2,1)S(1)} %pack_rows.1), channel_id=1, replica_groups=mesh['plant'=8,'feat'=8,'samp'=8] {'plant'}, dimensions={0} | all-to-all | bytes 2228224 | tf_op jit(solution)/shard_map/all_to_all | solution.py:198
  41.8 0.0 copy-done
  41.8 0.4 take_rows.1
  42.2 11.2 %all_to_all.31.got_ref = f32[8,1,1024]{2,1,0:T(1,128)S(1)} all-to-all(f32[8,1,1024]{2,1,0:T(1,128)S(1)} %get-tuple-element.15), channel_id=1, replica_groups=mesh['plant'=8,'feat'=8,'samp'=8] {'feat'}, dimensions={0} | all-to-all | bytes 65536 | tf_op jit(solution)/shard_map/all_to_all | solution.py:198
  53.4 0.2 to_residual.1
  53.7 13.3 %all_to_all.32.got_ref = f32[8,1,640]{2,1,0:T(1,128)S(1)} all-to-all(f32[8,1,640]{2,1,0:T(1,128)S(1)} %get-tuple-element.18), channel_id=1, replica_groups=mesh['plant'=8,'feat'=8,'samp'=8] {'samp'}, dimensions={0} | all-to-all | bytes 40960 | tf_op jit(solution)/shard_map/all_to_all | solution.py:198
  67.0 0.4 to_direction.1
  67.3 9.3 %all_to_all.33.got_ref = f32[8,1,1152]{2,1,0:T(1,128)S(1)} all-to-all(f32[8,1,1152]{2,1,0:T(1,128)S(1)} %get-tuple-element.19), channel_id=1, replica_groups=mesh['plant'=8,'feat'=8,'samp'=8] {'feat'}, dimensions={0} | all-to-all | bytes 73728 | tf_op jit(solution)/shard_map/all_to_all | solution.py:198
  76.6 0.2 to_image.1
  76.9 9.5 %all_to_all.34.got_ref = f32[8,1,1664]{2,1,0:T(1,128)S(1)} all-to-all(f32[8,1,1664]{2,1,0:T(1,128)S(1)} %get-tuple-element.21), channel_id=1, replica_groups=mesh['plant'=8,'feat'=8,'samp'=8] {'samp'}, dimensions={0} | all-to-all | bytes 106496 | tf_op jit(solution)/shard_map/all_to_all | solution.py:198
  86.4 1.1 %to_second.1 = (f32[1,512]{1,0:T(1,128)S(1)}, f32[1,128]{1,0:T(1,128)S(1)}, bf16[64,8,128]{2,1,0:T(8,128)(2,1)}) custom-call(f32[8,1,1664]{2,1,0:T(1,128)S(1)} %all_to_all.34.got_ref, f32[1,128]{1,0:T(1,128)S(1)} %get-tuple-element.22.sq_norm_ref, f32[1,1024]{1,0:T(1,128)S(1)} %get-tuple-element.20.curv_ref, f32[1,512]{1,0:T(1,128)S(1)} %get-tuple-element.23.grad_ref, ...), custom_call_target="tpu_custom_call" | custom-call | tf_op jit(solution)/shard_map/to_second/pallas_call | solution.py:54
  87.5 5.9 %all-to-all-start.5 = ((bf16[64,8,128]{2,1,0:T(8,128)(2,1)}), bf16[64,8,128]{2,1,0:T(8,128)(2,1)S(1)}, u32[]{:S(2)}, u32[]{:S(2)}) async-start(bf16[64,8,128]{2,1,0:T(8,128)(2,1)} %get-tuple-element.25), calls=%async_computation.5 | async-start | bytes 262144 | tf_op jit(solution)/shard_map/all_to_all | solution.py:198
  93.4 0.1 constant_dynamic-slice_fusion.1.grad_ref
  93.5 0.0 copy-start.1
  93.5 0.1 constant_dynamic-slice_fusion.resid_ref
  93.6 9.9 %all-to-all-done.5.got_ref = bf16[64,8,128]{2,1,0:T(8,128)(2,1)S(1)} async-done(((bf16[64,8,128]{2,1,0:T(8,128)(2,1)}), bf16[64,8,128]{2,1,0:T(8,128)(2,1)S(1)}, u32[]{:S(2)}, u32[]{:S(2)}) %all-to-all-start.5) | async-done | bytes 131104 | tf_op jit(solution)/shard_map/all_to_all | solution.py:198
  103.4 0.7 to_step.1
  104.1 0.0 copy-done.1
  (1 shorter events, 0.0 us)
Async XLA Ops:
  2.5 39.3 %copy-start = (f32[1,512]{1,0:T(1,128)S(1)}, f32[1,512]{1,0:T(1,128)}, u32[]{:S(2)}) copy-start(f32[1,512]{1,0:T(1,128)} %w_ref.3) | copy-start | bytes 6148
  87.5 15.9 %all-to-all-start.5 = ((bf16[64,8,128]{2,1,0:T(8,128)(2,1)}), bf16[64,8,128]{2,1,0:T(8,128)(2,1)S(1)}, u32[]{:S(2)}, u32[]{:S(2)}) async-start(bf16[64,8,128]{2,1,0:T(8,128)(2,1)} %get-tuple-element.25), calls=%async_computation.5 | async-start | bytes 262144 | tf_op jit(solution)/shard_map/all_to_all | solution.py:198
  93.5 10.7 %copy-start.1 = (f32[1,64]{1,0:T(1,128)}, f32[1,64]{1,0:T(1,128)S(1)}, u32[]{:S(2)}) copy-start(f32[1,64]{1,0:T(1,128)S(1)} %constant_dynamic-slice_fusion.1.grad_ref) | copy-start | bytes 772

commit v4 on v2

--- a/solution.py
+++ b/solution.py
@@ -50,11 +50,12 @@
     return jnp.sum(row, axis=1, keepdims=True)
 
 
-def call(kernel, *args, out):
+def call(kernel, *args, out, scratch=(), space=pltpu.VMEM):
     return pl.pallas_call(
         kernel,
         out_shape=out,
-        in_specs=[pl.BlockSpec(memory_space=pltpu.VMEM)] * len(args),
+        in_specs=[pl.BlockSpec(memory_space=space)] * len(args),
+        scratch_shapes=scratch,
         out_specs=jax.tree.map(lambda _: pl.BlockSpec(memory_space=pltpu.VMEM), out),
         compiler_params=pltpu.CompilerParams(vmem_limit_bytes=GRANT),
         name=kernel.func.__name__ if isinstance(kernel, functools.partial) else kernel.__name__,
@@ -65,20 +66,31 @@
     return jax.ShapeDtypeStruct(dims, dtype)
 
 
-def pack_rows(cap, ids_ref, lab_ref, emb_ref, out_ref):
+def pack_rows(cap, ids_in, lab_in, emb_in, out_ref, ids_ref, lab_ref, emb_ref, sems):
+    copies = [
+        pltpu.make_async_copy(src, dst, sems.at[k])
+        for k, (src, dst) in enumerate(
+            ((ids_in, ids_ref), (lab_in, lab_ref), (emb_in, emb_ref))
+        )
+    ]
+    for copy in copies:
+        copy.start()
     rows = emb_ref.shape[0]
-    ids = ids_ref[...]
     heads = lax.broadcasted_iota(jnp.int32, (PEERS, rows), 0)
-    members = heads == ids
-    mem_f = members.astype(f32)
     earlier = lax.broadcasted_iota(jnp.int32, (rows, rows), 0) < lax.broadcasted_iota(
         jnp.int32, (rows, rows), 1
     )
-    before = nn(mem_f.astype(bf16), earlier.astype(f32).astype(bf16))
+    earlier = earlier.astype(f32).astype(bf16)
+    copies[0].wait()
+    copies[1].wait()
+    ids = ids_ref[...]
+    mem_f = (heads == ids).astype(f32)
+    before = nn(mem_f.astype(bf16), earlier)
     rank = jnp.sum(before * mem_f, axis=0, keepdims=True).astype(jnp.int32)
     at_rank = lax.broadcasted_iota(jnp.int32, (cap, rows), 0) == rank
     tags = (lab_ref[...] + 1).astype(f32)
     tag_slots = nt((mem_f * tags).astype(bf16), at_rank.astype(f32).astype(bf16))
+    copies[2].wait()
     emb = emb_ref[...]
     for p in range(PEERS):
         pick = (at_rank & (ids == p)).astype(f32).astype(bf16)
@@ -105,13 +117,20 @@
     send(out_ref, part, lanes(row_sum(valid.astype(f32))))
 
 
-def to_direction(got_ref, w_ref, rows_ref, grad_ref, count_ref, out_ref):
+def own_share(row, share):
+    width = row.shape[1]
+    at = lax.axis_index("samp") * share
+    return pltpu.roll(row, lax.rem(width - at, width), 1)[:, :share]
+
+
+def to_direction(got_ref, w_ref, rows_ref, grad_ref, count_ref, share_ref, out_ref):
     width = rows_ref.shape[1]
     total = total_of(got_ref)
     count = total[:, width : width + 1]
     grad = total[:, :width] / count + penalty * w_ref[...]
     grad_ref[...] = grad
     count_ref[...] = lanes(count)
+    share_ref[...] = own_share(grad, share_ref.shape[1])
     part = nt(rep(-grad).astype(bf16), rows_ref[...])[:1]
     send(out_ref, part, lanes(row_sum(grad * grad)))
 
@@ -126,7 +145,7 @@
     send(out_ref, part, lanes(row_sum(weighted * proj)))
 
 
-def to_second(got_ref, proj_ref, grad_ref, count_ref, rows_ref, resid_ref, step_ref, out_ref):
+def to_second(got_ref, proj_ref, grad_ref, count_ref, rows_ref, keep_ref, out_ref):
     width, slots = rows_ref.shape[1], rows_ref.shape[0]
     total = total_of(got_ref)
     count = count_ref[:, :1]
@@ -135,8 +154,9 @@
     image = total[:, :width] / count + penalty * direction
     step = sq_norm / (total[:, width : width + 1] / count + penalty * sq_norm)
     resid = direction - step * image
-    resid_ref[...] = resid
-    step_ref[...] = lanes(step)
+    share = keep_ref.shape[1] - LANES
+    keep_ref[:, :LANES] = lanes(step)
+    keep_ref[:, LANES:] = own_share(resid, share)
     part = nt(rep(resid).astype(bf16), rows_ref[...])[:1]
     send(out_ref, part, lanes(row_sum(resid * resid)), lanes(row_sum(resid * direction)))
 
@@ -157,14 +177,15 @@
     keep_ref[:, 2 * LANES :] = lanes(dir_sq)
 
 
-def to_step(got_ref, count_ref, keep_ref, first_ref, grad_ref, resid_ref, out_ref):
-    beta = keep_ref[:, :1]
-    sq_next = keep_ref[:, LANES : LANES + 1]
-    dir_sq = keep_ref[:, 2 * LANES : 2 * LANES + 1]
+def to_step(got_ref, count_ref, scalars_ref, first_ref, grad_ref, out_ref):
+    beta = scalars_ref[:, :1]
+    sq_next = scalars_ref[:, LANES : LANES + 1]
+    dir_sq = scalars_ref[:, 2 * LANES : 2 * LANES + 1]
     bend = total_of(got_ref)[:, :1]
     step = sq_next / (bend / count_ref[:, :1] + penalty * dir_sq)
     direction = -grad_ref[...]
-    out_ref[...] = first_ref[:, :1] * direction + step * (resid_ref[...] + beta * direction)
+    resid = first_ref[:, LANES:]
+    out_ref[...] = first_ref[:, :1] * direction + step * (resid + beta * direction)
 
 
 def exchange(values, axis):
@@ -177,14 +198,21 @@
     share = width // samps
     cap = 2 * rows_here // PEERS
     slots = PEERS * cap
-    at = lax.axis_index("samp") * share
 
     sent = call(
         functools.partial(pack_rows, cap),
-        plant_ids.reshape(1, rows_here),
-        labels.reshape(1, rows_here),
-        embeddings,
+        *(
+            pltpu.with_memory_space_constraint(v, pltpu.HBM)
+            for v in (plant_ids.reshape(1, rows_here), labels.reshape(1, rows_here), embeddings)
+        ),
         out=shape(PEERS, cap + PEERS, width, dtype=bf16),
+        scratch=(
+            pltpu.VMEM((1, rows_here), jnp.int32),
+            pltpu.VMEM((1, rows_here), jnp.int32),
+            pltpu.VMEM((rows_here, width), bf16),
+            pltpu.SemaphoreType.DMA((3,)),
+        ),
+        space=pltpu.HBM,
     )
     got = exchange(sent, "plant")
     rows, tags, part = call(
@@ -198,43 +226,39 @@
         to_residual, got, tags, rows, out=(shape(1, slots), shape(PEERS, 1, width + LANES))
     )
     got = exchange(part, "samp")
-    grad, count, part = call(
+    grad, count, grad_share, part = call(
         to_direction,
         got,
         weights,
         rows,
-        out=(shape(1, width), shape(1, LANES), shape(PEERS, 1, slots + LANES)),
+        out=(
+            shape(1, width),
+            shape(1, LANES),
+            shape(1, share),
+            shape(PEERS, 1, slots + LANES),
+        ),
     )
     got = exchange(part, "feat")
     proj, part = call(
         to_image, got, curv, rows, out=(shape(1, slots + LANES), shape(PEERS, 1, width + LANES))
     )
     got = exchange(part, "samp")
-    resid, first, part = call(
+    first, part = call(
         to_second,
         got,
         proj,
         grad,
         count,
         rows,
-        out=(shape(1, width), shape(1, LANES), shape(PEERS, 1, slots + 2 * LANES)),
+        out=(shape(1, LANES + share), shape(PEERS, 1, slots + 2 * LANES)),
     )
     got = exchange(part, "feat")
     scalars, part = call(
         to_bend, got, proj, curv, out=(shape(1, 3 * LANES), shape(PEERS, 1, LANES))
     )
     got = exchange(part, "samp")
-    grad_share = lax.dynamic_slice_in_dim(grad, at, share, 1)
-    resid_share = lax.dynamic_slice_in_dim(resid, at, share, 1)
     newton_step = call(
-        to_step,
-        got,
-        count,
-        scalars,
-        first,
-        grad_share,
-        resid_share,
-        out=shape(1, share),
+        to_step, got, count, scalars, first, grad_share, out=shape(1, share)
     )
     return newton_step, grad_share
 

time: 111 us -> 106 us (0.955)
  blocking collectives: 73.1 us -> 100 us
  waiting for transfers between devices: 17.6 us -> 0 us
  starting transfers between devices: 11.7 us -> 0 us
  local copies, waits for them, and re-layouts: 2.56 us -> 0.01 us
    all_to_all x4 -> x7, blocking collectives: 73.1 us -> 100 us  [exchange(): return lax.all_to_all(values, axis, split_axis=0, concat_axis=0, tiled=True)]
    all_to_all x3 -> x0, waiting for transfers between devices: 17.6 us -> none  [exchange(): return lax.all_to_all(values, axis, split_axis=0, concat_axis=0, tiled=True)]
    all_to_all x3 -> x0, starting transfers between devices: 11.7 us -> none  [exchange(): return lax.all_to_all(values, axis, split_axis=0, concat_axis=0, tiled=True)]
    unnamed x10 -> x4, local copies, waits for them, and re-layouts: 2.41 us -> 0.01 us
  transfers between devices with their start and end apart: 3 -> 0, of which waited for: 3 -> 0; matrix products, arithmetic and copies ran while one was open for 0% -> 0% of each run, Pallas kernels for 0% -> 0%
where the time goes in v4:
time: 106 us; the launch traced here: 105 us
  blocking collectives  100 us (94%)
  Pallas kernels  4.55 us (4%)
    all_to_all x7, blocking collectives, exchange(): return lax.all_to_all(values, axis, split_axis=0, concat_axis=0, tiled=True)  100 us
    pallas_call x8, Pallas kernels, call(): pl.pallas_call(kernel, out_shape=out, in_specs=[pl.BlockSpec(memory_space...  4.55 us

profile of v4, /device:TPU:1, one launch (start us, length us, event | category | flops | bytes accessed | tf_op | source)
XLA Modules:
  0.0 105.2 jit_solution(15293147244518378833)
XLA Ops:
  0.6 1.8 %pack_rows.1 = bf16[8,136,512]{2,1,0:T(8,128)(2,1)S(1)} custom-call(s32[1,512]{1,0:T(1,128)} %bitcast.2, s32[1,512]{1,0:T(1,128)} %bitcast.3, bf16[512,512]{1,0:T(8,128)(2,1)} %emb_in.1), custom_call_target="tpu_custom_call" | custom-call | tf_op jit(solution)/shard_map/pack_rows/pallas_call | solution.py:54
  2.5 0.0 copy-start
  2.5 39.3 %all_to_all.35.got_ref = bf16[8,136,512]{2,1,0:T(8,128)(2,1)S(1)} all-to-all(bf16[8,136,512]{2,1,0:T(8,128)(2,1)S(1)} %pack_rows.1), channel_id=1, replica_groups=mesh['plant'=8,'feat'=8,'samp'=8] {'plant'}, dimensions={0} | all-to-all | bytes 2228224 | tf_op jit(solution)/shard_map/all_to_all | solution.py:192
  41.8 0.0 copy-done
  41.8 0.4 take_rows.1
  42.2 11.2 %all_to_all.36.got_ref = f32[8,1,1024]{2,1,0:T(1,128)S(1)} all-to-all(f32[8,1,1024]{2,1,0:T(1,128)S(1)} %get-tuple-element.17), channel_id=1, replica_groups=mesh['plant'=8,'feat'=8,'samp'=8] {'feat'}, dimensions={0} | all-to-all | bytes 65536 | tf_op jit(solution)/shard_map/all_to_all | solution.py:192
  53.4 0.2 to_residual.1
  53.7 13.3 %all_to_all.37.got_ref = f32[8,1,640]{2,1,0:T(1,128)S(1)} all-to-all(f32[8,1,640]{2,1,0:T(1,128)S(1)} %get-tuple-element.20), channel_id=1, replica_groups=mesh['plant'=8,'feat'=8,'samp'=8] {'samp'}, dimensions={0} | all-to-all | bytes 40960 | tf_op jit(solution)/shard_map/all_to_all | solution.py:192
  67.0 0.7 to_direction.1
  67.6 9.3 %all_to_all.38.got_ref = f32[8,1,1152]{2,1,0:T(1,128)S(1)} all-to-all(f32[8,1,1152]{2,1,0:T(1,128)S(1)} %get-tuple-element.21), channel_id=1, replica_groups=mesh['plant'=8,'feat'=8,'samp'=8] {'feat'}, dimensions={0} | all-to-all | bytes 73728 | tf_op jit(solution)/shard_map/all_to_all | solution.py:192
  76.9 0.0 copy-start.1
  76.9 0.2 to_image.1
  77.1 9.0 %all_to_all.39.got_ref = f32[8,1,640]{2,1,0:T(1,128)S(1)} all-to-all(f32[8,1,640]{2,1,0:T(1,128)S(1)} %get-tuple-element.23), channel_id=1, replica_groups=mesh['plant'=8,'feat'=8,'samp'=8] {'samp'}, dimensions={0} | all-to-all | bytes 40960 | tf_op jit(solution)/shard_map/all_to_all | solution.py:192
  86.1 0.4 to_second.1
  86.5 9.0 %all_to_all.40.got_ref = f32[8,1,1280]{2,1,0:T(1,128)S(1)} all-to-all(f32[8,1,1280]{2,1,0:T(1,128)S(1)} %get-tuple-element.27), channel_id=1, replica_groups=mesh['plant'=8,'feat'=8,'samp'=8] {'feat'}, dimensions={0} | all-to-all | bytes 81920 | tf_op jit(solution)/shard_map/all_to_all | solution.py:192
  95.5 0.2 to_bend.1
  95.7 8.9 %all_to_all.41.got_ref = f32[8,1,128]{2,1,0:T(1,128)S(1)} all-to-all(f32[8,1,128]{2,1,0:T(1,128)S(1)} %get-tuple-element.28), channel_id=1, replica_groups=mesh['plant'=8,'feat'=8,'samp'=8] {'samp'}, dimensions={0} | all-to-all | bytes 8192 | tf_op jit(solution)/shard_map/all_to_all | solution.py:192
  104.6 0.0 copy-done.1
  104.6 0.6 to_step.1
Async XLA Ops:
  2.5 39.3 %copy-start = (f32[1,512]{1,0:T(1,128)S(1)}, f32[1,512]{1,0:T(1,128)}, u32[]{:S(2)}) copy-start(f32[1,512]{1,0:T(1,128)} %w_ref.3) | copy-start | bytes 6148
  76.9 27.7 %copy-start.1 = (f32[1,64]{1,0:T(1,128)S(1)}, f32[1,64]{1,0:T(1,128)}, u32[]{:S(2)}) copy-start(f32[1,64]{1,0:T(1,128)} %get-tuple-element.16.grad_ref) | copy-start | bytes 772

commit v5 on v3

--- a/solution.py
+++ b/solution.py
@@ -10,6 +10,7 @@
 penalty = 0.1
 PEERS = 8
 LANES = 128
+DEEP = 16
 GRANT = 12 << 20
 f32 = jnp.float32
 bf16 = jnp.bfloat16
@@ -92,17 +93,30 @@
     tag_slots = nt((mem_f * tags).astype(bf16), at_rank.astype(f32).astype(bf16))
     copies[2].wait()
     emb = emb_ref[...]
+    across = emb.shape[1] // LANES
     for p in range(PEERS):
         pick = (at_rank & (ids == p)).astype(f32).astype(bf16)
-        out_ref[p, :cap, :] = nn(pick, emb).astype(bf16)
-        out_ref[p, cap:, :cap] = jnp.broadcast_to(tag_slots[p : p + 1], (PEERS, cap)).astype(bf16)
-        out_ref[p, cap:, cap:] = jnp.zeros((PEERS, rows - cap), bf16)
+        picked = nn(pick, emb).astype(bf16)
+        for down in range(cap // DEEP):
+            for over in range(across):
+                out_ref[p, down * across + over] = picked[
+                    down * DEEP : (down + 1) * DEEP, over * LANES : (over + 1) * LANES
+                ]
+        out_ref[p, cap // DEEP * across] = jnp.broadcast_to(
+            tag_slots[p : p + 1], (DEEP, cap)
+        ).astype(bf16)
 
 
 def take_rows(cap, got_ref, w_ref, rows_ref, tags_ref, out_ref):
+    across = rows_ref.shape[1] // LANES
     for p in range(PEERS):
-        rows_ref[p * cap : (p + 1) * cap, :] = got_ref[p, :cap, :]
-        tags_ref[:, p * cap : (p + 1) * cap] = got_ref[p, cap:, :cap].astype(f32)[:1]
+        for down in range(cap // DEEP):
+            for over in range(across):
+                at = p * cap + down * DEEP
+                rows_ref[at : at + DEEP, over * LANES : (over + 1) * LANES] = got_ref[
+                    p, down * across + over
+                ]
+        tags_ref[:, p * cap : (p + 1) * cap] = got_ref[p, cap // DEEP * across].astype(f32)[:1]
     send(out_ref, nt(rep(w_ref[...]).astype(bf16), rows_ref[...])[:1])
 
 
@@ -117,13 +131,20 @@
     send(out_ref, part, lanes(row_sum(valid.astype(f32))))
 
 
-def to_direction(got_ref, w_ref, rows_ref, grad_ref, count_ref, out_ref):
+def own_share(row, share):
+    width = row.shape[1]
+    at = lax.axis_index("samp") * share
+    return pltpu.roll(row, lax.rem(width - at, width), 1)[:, :share]
+
+
+def to_direction(got_ref, w_ref, rows_ref, grad_ref, count_ref, share_ref, out_ref):
     width = rows_ref.shape[1]
     total = total_of(got_ref)
     count = total[:, width : width + 1]
     grad = total[:, :width] / count + penalty * w_ref[...]
     grad_ref[...] = grad
     count_ref[...] = lanes(count)
+    share_ref[...] = own_share(grad, share_ref.shape[1])
     part = nt(rep(-grad).astype(bf16), rows_ref[...])[:1]
     send(out_ref, part, lanes(row_sum(grad * grad)))
 
@@ -139,7 +160,7 @@
     send(out_ref, part, lanes(row_sum(weighted * proj)), jnp.sqrt(curv) * proj)
 
 
-def to_second(got_ref, sq_norm_ref, curv_ref, grad_ref, count_ref, rows_ref, resid_ref, step_ref, out_ref):
+def to_second(got_ref, sq_norm_ref, curv_ref, grad_ref, count_ref, rows_ref, keep_ref, out_ref):
     width, cap = rows_ref.shape[1], rows_ref.shape[0] // PEERS
     total = got_ref[0, :, : width + LANES]
     for p in range(1, PEERS):
@@ -150,8 +171,8 @@
     image = total[:, :width] / count + penalty * direction
     step = sq_norm / (total[:, width : width + 1] / count + penalty * sq_norm)
     resid = direction - step * image
-    resid_ref[...] = resid
-    step_ref[...] = lanes(step)
+    keep_ref[:, :LANES] = lanes(step)
+    keep_ref[:, LANES:] = own_share(resid, keep_ref.shape[1] - LANES)
     part = nt(rep(resid).astype(bf16), rows_ref[...]) * jnp.sqrt(curv_ref[...])
     source = lax.broadcasted_iota(jnp.int32, (PEERS, cap), 0)
     tile = part[:, :cap]
@@ -162,20 +183,16 @@
         out_ref[peer] = tile
 
 
-def to_tiles(got_ref, out_ref):
-    groups, cap = out_ref.shape[0], out_ref.shape[2]
-    start = got_ref.shape[2] - PEERS * cap
+def to_step(got_ref, first_ref, count_ref, sq_norm_ref, keep_ref, share_ref, out_ref, grad_ref, tiles_ref):
+    groups, _, cap = tiles_ref.shape
+    feats = got_ref.shape[0] // groups
+    start = first_ref.shape[2] - PEERS * cap
     for s in range(groups):
         for p in range(PEERS):
-            out_ref[s, p : p + 1, :] = got_ref[s, :, start + p * cap : start + (p + 1) * cap]
-
-
-def to_step(got_ref, first_ref, count_ref, sq_norm_ref, step_ref, grad_ref, resid_ref, out_ref):
-    groups = first_ref.shape[0]
-    feats = got_ref.shape[0] // groups
+            tiles_ref[s, p : p + 1, :] = first_ref[s, :, start + p * cap : start + (p + 1) * cap]
     first_sq, cross, second_sq = 0.0, 0.0, 0.0
     for s in range(groups):
-        first = first_ref[s]
+        first = tiles_ref[s]
         second = got_ref[s].astype(f32)
         for f in range(1, feats):
             second = second + got_ref[f * groups + s].astype(f32)
@@ -185,13 +202,14 @@
     first_sq, cross, second_sq = (
         jnp.sum(row_sum(v), axis=0, keepdims=True) for v in (first_sq, cross, second_sq)
     )
-    count, sq_norm, first_step = count_ref[:, :1], sq_norm_ref[:, :1], step_ref[:, :1]
+    count, sq_norm, first_step = count_ref[:, :1], sq_norm_ref[:, :1], keep_ref[:, :1]
     sq_next = -first_step * cross / count
     beta = sq_next / sq_norm
     bend = second_sq + 2.0 * beta * cross + beta * beta * first_sq
     step = sq_next / (bend / count + penalty * (sq_next + beta * beta * sq_norm))
-    direction = -grad_ref[...]
-    out_ref[...] = first_step * direction + step * (resid_ref[...] + beta * direction)
+    grad_ref[...] = share_ref[...]
+    direction = -share_ref[...]
+    out_ref[...] = first_step * direction + step * (keep_ref[:, LANES:] + beta * direction)
 
 
 def exchange(values, axis):
@@ -204,7 +222,6 @@
     share = width // samps
     cap = 2 * rows_here // PEERS
     slots = PEERS * cap
-    at = lax.axis_index("samp") * share
 
     sent = call(
         functools.partial(pack_rows, cap),
@@ -212,7 +229,7 @@
             pltpu.with_memory_space_constraint(v, pltpu.HBM)
             for v in (plant_ids.reshape(1, rows_here), labels.reshape(1, rows_here), embeddings)
         ),
-        out=shape(PEERS, cap + PEERS, width, dtype=bf16),
+        out=shape(PEERS, cap // DEEP * (width // LANES) + 1, DEEP, LANES, dtype=bf16),
         scratch=(
             pltpu.VMEM((1, rows_here), jnp.int32),
             pltpu.VMEM((1, rows_here), jnp.int32),
@@ -233,52 +250,52 @@
         to_residual, got, tags, rows, out=(shape(1, slots), shape(PEERS, 1, width + LANES))
     )
     got = exchange(part, "samp")
-    grad, count, part = call(
+    grad, count, grad_share, part = call(
         to_direction,
         got,
         weights,
         rows,
-        out=(shape(1, width), shape(1, LANES), shape(PEERS, 1, slots + LANES)),
+        out=(
+            shape(1, width),
+            shape(1, LANES),
+            shape(1, share),
+            shape(PEERS, 1, slots + LANES),
+        ),
     )
     got = exchange(part, "feat")
-    sq_norm, part = call(
+    sq_norm, first = call(
         to_image,
         got,
         curv,
         rows,
         out=(shape(1, LANES), shape(PEERS, 1, width + LANES + slots)),
     )
-    got = exchange(part, "samp")
-    resid, first_step, part = call(
+    first = exchange(first, "samp")
+    keep, part = call(
         to_second,
-        got,
+        first,
         sq_norm,
         curv,
         grad,
         count,
         rows,
         out=(
-            shape(1, width),
-            shape(1, LANES),
+            shape(1, LANES + share),
             shape(lax.axis_size("feat") * samps, PEERS, cap, dtype=bf16),
         ),
     )
-    first = call(to_tiles, got, out=shape(samps, PEERS, cap))
     got = exchange(part, ("feat", "samp"))
-    grad_share = lax.dynamic_slice_in_dim(grad, at, share, 1)
-    resid_share = lax.dynamic_slice_in_dim(resid, at, share, 1)
-    newton_step = call(
+    return call(
         to_step,
         got,
         first,
         count,
         sq_norm,
-        first_step,
+        keep,
         grad_share,
-        resid_share,
-        out=shape(1, share),
-    )
-    return newton_step, grad_share
+        out=(shape(1, share), shape(1, share)),
+        scratch=(pltpu.VMEM((samps, PEERS, cap), f32),),
+    )
 
 
 def solution(mesh):

time: 105 us -> 102 us (0.971)
  blocking collectives: 82.6 us -> 97.1 us
  waiting for transfers between devices: 9.86 us -> 0 us
  starting transfers between devices: 5.91 us -> 0 us
    all_to_all x5 -> x6, blocking collectives: 82.6 us -> 97.1 us  [exchange(): return lax.all_to_all(values, axis, split_axis=0, concat_axis=0, tiled=True)]
    all_to_all x1 -> x0, waiting for transfers between devices: 9.86 us -> none  [exchange(): return lax.all_to_all(values, axis, split_axis=0, concat_axis=0, tiled=True)]
    all_to_all x1 -> x0, starting transfers between devices: 5.91 us -> none  [exchange(): return lax.all_to_all(values, axis, split_axis=0, concat_axis=0, tiled=True)]
    pallas_call x8 -> x7, Pallas kernels: 4.9 us -> 4.26 us  [call(): pl.pallas_call(kernel, out_shape=out, in_specs=[pl.BlockSpec(memory_space...]
  transfers between devices with their start and end apart: 1 -> 0, of which waited for: 1 -> 0; matrix products, arithmetic and copies ran while one was open for 0% -> 0% of each run, Pallas kernels for 0% -> 0%
where the time goes in v5:
time: 102 us
  blocking collectives  97.1 us (95%)
  Pallas kernels  4.26 us (4%)
    all_to_all x6, blocking collectives, exchange(): return lax.all_to_all(values, axis, split_axis=0, concat_axis=0, tiled=True)  97.1 us
    pallas_call x7, Pallas kernels, call(): pl.pallas_call(kernel, out_shape=out, in_specs=[pl.BlockSpec(memory_space...  4.26 us

profile of v5, /device:TPU:1, one launch (start us, length us, event | category | flops | bytes accessed | tf_op | source)
XLA Modules:
  0.0 102.0 jit_solution(1600440448770873325)
XLA Ops:
  0.6 1.8 %pack_rows.1 = bf16[8,33,16,128]{3,2,1,0:T(8,128)(2,1)S(1)} custom-call(s32[1,512]{1,0:T(1,128)} %bitcast.2, s32[1,512]{1,0:T(1,128)} %bitcast.3, bf16[512,512]{1,0:T(8,128)(2,1)} %emb_in.1), custom_call_target="tpu_custom_call" | custom-call | tf_op jit(solution)/shard_map/pack_rows/pallas_call | solution.py:55
  2.5 0.0 copy-start
  2.5 38.4 %all_to_all.30.got_ref = bf16[8,33,16,128]{3,2,1,0:T(8,128)(2,1)S(1)} all-to-all(bf16[8,33,16,128]{3,2,1,0:T(8,128)(2,1)S(1)} %pack_rows.1), channel_id=1, replica_groups=mesh['plant'=8,'feat'=8,'samp'=8] {'plant'}, dimensions={0} | all-to-all | bytes 2162688 | tf_op jit(solution)/shard_map/all_to_all | solution.py:216
  40.9 0.0 copy-done
  40.9 0.4 take_rows.1
  41.3 11.5 %all_to_all.31.got_ref = f32[8,1,1024]{2,1,0:T(1,128)S(1)} all-to-all(f32[8,1,1024]{2,1,0:T(1,128)S(1)} %get-tuple-element.15), channel_id=1, replica_groups=mesh['plant'=8,'feat'=8,'samp'=8] {'feat'}, dimensions={0} | all-to-all | bytes 65536 | tf_op jit(solution)/shard_map/all_to_all | solution.py:216
  52.8 0.2 to_residual.1
  53.0 13.3 %all_to_all.32.got_ref = f32[8,1,640]{2,1,0:T(1,128)S(1)} all-to-all(f32[8,1,640]{2,1,0:T(1,128)S(1)} %get-tuple-element.18), channel_id=1, replica_groups=mesh['plant'=8,'feat'=8,'samp'=8] {'samp'}, dimensions={0} | all-to-all | bytes 40960 | tf_op jit(solution)/shard_map/all_to_all | solution.py:216
  66.3 0.4 to_direction.1
  66.7 9.3 %all_to_all.33.got_ref = f32[8,1,1152]{2,1,0:T(1,128)S(1)} all-to-all(f32[8,1,1152]{2,1,0:T(1,128)S(1)} %get-tuple-element.19), channel_id=1, replica_groups=mesh['plant'=8,'feat'=8,'samp'=8] {'feat'}, dimensions={0} | all-to-all | bytes 73728 | tf_op jit(solution)/shard_map/all_to_all | solution.py:216
  75.9 0.2 to_image.1
  76.2 9.5 %all_to_all.34.got_ref.first_ref = f32[8,1,1664]{2,1,0:T(1,128)S(1)} all-to-all(f32[8,1,1664]{2,1,0:T(1,128)S(1)} %get-tuple-element.21), channel_id=1, replica_groups=mesh['plant'=8,'feat'=8,'samp'=8] {'samp'}, dimensions={0} | all-to-all | bytes 106496 | tf_op jit(solution)/shard_map/all_to_all | solution.py:216
  85.7 0.4 to_second.1
  86.2 15.1 %all_to_all.35.got_ref = bf16[64,8,128]{2,1,0:T(8,128)(2,1)S(1)} all-to-all(bf16[64,8,128]{2,1,0:T(8,128)(2,1)S(1)} %get-tuple-element.25), channel_id=1, replica_groups=mesh['plant'=8,'feat'=8,'samp'=8] {'feat','samp'}, dimensions={0} | all-to-all | bytes 262144 | tf_op jit(solution)/shard_map/all_to_all | solution.py:216
  101.3 0.7 to_step.1
Async XLA Ops:
  2.5 38.4 %copy-start = (f32[1,512]{1,0:T(1,128)S(1)}, f32[1,512]{1,0:T(1,128)}, u32[]{:S(2)}) copy-start(f32[1,512]{1,0:T(1,128)} %w_ref.3) | copy-start | bytes 6148

commit v6 on v5

--- a/solution.py
+++ b/solution.py
@@ -203,10 +203,11 @@
         jnp.sum(row_sum(v), axis=0, keepdims=True) for v in (first_sq, cross, second_sq)
     )
     count, sq_norm, first_step = count_ref[:, :1], sq_norm_ref[:, :1], keep_ref[:, :1]
-    sq_next = -first_step * cross / count
+    sq_next = jnp.maximum(-first_step * cross / count, 0.0)
     beta = sq_next / sq_norm
-    bend = second_sq + 2.0 * beta * cross + beta * beta * first_sq
-    step = sq_next / (bend / count + penalty * (sq_next + beta * beta * sq_norm))
+    bend = jnp.maximum(second_sq + 2.0 * beta * cross + beta * beta * first_sq, 0.0)
+    below = bend / count + penalty * (sq_next + beta * beta * sq_norm)
+    step = jnp.where(sq_next > 0.0, sq_next / jnp.where(sq_next > 0.0, below, 1.0), 0.0)
     grad_ref[...] = share_ref[...]
     direction = -share_ref[...]
     out_ref[...] = first_step * direction + step * (keep_ref[:, LANES:] + beta * direction)

time: 102 us -> 102 us (level)
  no operation moved by 1% of the time
where the time goes in v6:
time: 102 us
  blocking collectives  97.1 us (95%)
  Pallas kernels  4.27 us (4%)
    all_to_all x6, blocking collectives, exchange(): return lax.all_to_all(values, axis, split_axis=0, concat_axis=0, tiled=True)  97.1 us
    pallas_call x7, Pallas kernels, call(): pl.pallas_call(kernel, out_shape=out, in_specs=[pl.BlockSpec(memory_space...  4.27 us

profile of v6, /device:TPU:1, one launch (start us, length us, event | category | flops | bytes accessed | tf_op | source)
XLA Modules:
  0.0 102.0 jit_solution(4378478130677270700)
XLA Ops:
  0.6 1.8 %pack_rows.1 = bf16[8,33,16,128]{3,2,1,0:T(8,128)(2,1)S(1)} custom-call(s32[1,512]{1,0:T(1,128)} %bitcast.2, s32[1,512]{1,0:T(1,128)} %bitcast.3, bf16[512,512]{1,0:T(8,128)(2,1)} %emb_in.1), custom_call_target="tpu_custom_call" | custom-call | tf_op jit(solution)/shard_map/pack_rows/pallas_call | solution.py:55
  2.5 0.0 copy-start
  2.5 38.4 %all_to_all.30.got_ref = bf16[8,33,16,128]{3,2,1,0:T(8,128)(2,1)S(1)} all-to-all(bf16[8,33,16,128]{3,2,1,0:T(8,128)(2,1)S(1)} %pack_rows.1), channel_id=1, replica_groups=mesh['plant'=8,'feat'=8,'samp'=8] {'plant'}, dimensions={0} | all-to-all | bytes 2162688 | tf_op jit(solution)/shard_map/all_to_all | solution.py:217
  40.9 0.0 copy-done
  40.9 0.4 take_rows.1
  41.3 11.5 %all_to_all.31.got_ref = f32[8,1,1024]{2,1,0:T(1,128)S(1)} all-to-all(f32[8,1,1024]{2,1,0:T(1,128)S(1)} %get-tuple-element.15), channel_id=1, replica_groups=mesh['plant'=8,'feat'=8,'samp'=8] {'feat'}, dimensions={0} | all-to-all | bytes 65536 | tf_op jit(solution)/shard_map/all_to_all | solution.py:217
  52.8 0.2 to_residual.1
  53.0 13.3 %all_to_all.32.got_ref = f32[8,1,640]{2,1,0:T(1,128)S(1)} all-to-all(f32[8,1,640]{2,1,0:T(1,128)S(1)} %get-tuple-element.18), channel_id=1, replica_groups=mesh['plant'=8,'feat'=8,'samp'=8] {'samp'}, dimensions={0} | all-to-all | bytes 40960 | tf_op jit(solution)/shard_map/all_to_all | solution.py:217
  66.3 0.4 to_direction.1
  66.7 9.3 %all_to_all.33.got_ref = f32[8,1,1152]{2,1,0:T(1,128)S(1)} all-to-all(f32[8,1,1152]{2,1,0:T(1,128)S(1)} %get-tuple-element.19), channel_id=1, replica_groups=mesh['plant'=8,'feat'=8,'samp'=8] {'feat'}, dimensions={0} | all-to-all | bytes 73728 | tf_op jit(solution)/shard_map/all_to_all | solution.py:217
  75.9 0.2 to_image.1
  76.2 9.5 %all_to_all.34.got_ref.first_ref = f32[8,1,1664]{2,1,0:T(1,128)S(1)} all-to-all(f32[8,1,1664]{2,1,0:T(1,128)S(1)} %get-tuple-element.21), channel_id=1, replica_groups=mesh['plant'=8,'feat'=8,'samp'=8] {'samp'}, dimensions={0} | all-to-all | bytes 106496 | tf_op jit(solution)/shard_map/all_to_all | solution.py:217
  85.7 0.4 to_second.1
  86.2 15.1 %all_to_all.35.got_ref = bf16[64,8,128]{2,1,0:T(8,128)(2,1)S(1)} all-to-all(bf16[64,8,128]{2,1,0:T(8,128)(2,1)S(1)} %get-tuple-element.25), channel_id=1, replica_groups=mesh['plant'=8,'feat'=8,'samp'=8] {'feat','samp'}, dimensions={0} | all-to-all | bytes 262144 | tf_op jit(solution)/shard_map/all_to_all | solution.py:217
  101.3 0.7 to_step.1
Async XLA Ops:
  2.5 38.4 %copy-start = (f32[1,512]{1,0:T(1,128)S(1)}, f32[1,512]{1,0:T(1,128)}, u32[]{:S(2)}) copy-start(f32[1,512]{1,0:T(1,128)} %w_ref.3) | copy-start | bytes 6148

commit v7 on v6

--- a/solution.py
+++ b/solution.py
@@ -149,60 +149,62 @@
     send(out_ref, part, lanes(row_sum(grad * grad)))
 
 
-def to_image(got_ref, curv_ref, rows_ref, sq_norm_ref, out_ref):
+def to_image(got_ref, curv_ref, rows_ref, proj_ref, out_ref):
     slots = rows_ref.shape[0]
     total = total_of(got_ref)
-    sq_norm_ref[...] = total[:, slots:]
+    proj_ref[...] = total
     proj = total[:, :slots]
-    curv = curv_ref[...]
-    weighted = (curv * proj).astype(bf16).astype(f32)
+    weighted = (curv_ref[...] * proj).astype(bf16).astype(f32)
     part = nn(rep(weighted).astype(bf16), rows_ref[...])[:1]
-    send(out_ref, part, lanes(row_sum(weighted * proj)), jnp.sqrt(curv) * proj)
-
-
-def to_second(got_ref, sq_norm_ref, curv_ref, grad_ref, count_ref, rows_ref, keep_ref, out_ref):
-    width, cap = rows_ref.shape[1], rows_ref.shape[0] // PEERS
-    total = got_ref[0, :, : width + LANES]
-    for p in range(1, PEERS):
-        total = total + got_ref[p, :, : width + LANES]
+    send(out_ref, part, lanes(row_sum(weighted * proj)))
+
+
+def to_second(got_ref, proj_ref, curv_ref, grad_ref, count_ref, rows_ref, keep_ref, out_ref, pair_ref):
+    width, slots = rows_ref.shape[1], rows_ref.shape[0]
+    half = slots // 2
+    total = total_of(got_ref)
     count = count_ref[:, :1]
-    sq_norm = sq_norm_ref[:, :1]
+    sq_norm = proj_ref[:, slots : slots + 1]
     direction = -grad_ref[...]
     image = total[:, :width] / count + penalty * direction
-    step = sq_norm / (total[:, width : width + 1] / count + penalty * sq_norm)
+    bend = total[:, width : width + 1]
+    step = sq_norm / (bend / count + penalty * sq_norm)
     resid = direction - step * image
     keep_ref[:, :LANES] = lanes(step)
-    keep_ref[:, LANES:] = own_share(resid, keep_ref.shape[1] - LANES)
-    part = nt(rep(resid).astype(bf16), rows_ref[...]) * jnp.sqrt(curv_ref[...])
-    source = lax.broadcasted_iota(jnp.int32, (PEERS, cap), 0)
-    tile = part[:, :cap]
-    for p in range(1, PEERS):
-        tile = jnp.where(source == p, part[:, p * cap : (p + 1) * cap], tile)
-    tile = tile.astype(bf16)
+    keep_ref[:, LANES : 2 * LANES] = lanes(bend)
+    keep_ref[:, 2 * LANES : 3 * LANES] = lanes(sq_norm)
+    keep_ref[:, 3 * LANES :] = own_share(resid, keep_ref.shape[1] - 3 * LANES)
+    curv = curv_ref[...]
+    part = nt(rep(resid).astype(bf16), rows_ref[...])[:1]
+    cross = row_sum(curv * proj_ref[:, :slots] * part)
+    scaled = part * jnp.sqrt(curv)
+    first = cross.astype(bf16).astype(f32)
+    second = (cross - first).astype(bf16).astype(f32)
+    third = cross - first - second
+    lane = lax.broadcasted_iota(jnp.int32, (1, LANES), 1)
+    extra = jnp.where(lane == 0, first, jnp.where(lane == 1, second, jnp.where(lane == 2, third, 0.0)))
+    pair_ref[0:1, :half] = scaled[:, :half]
+    pair_ref[1:2, :half] = scaled[:, half:]
+    pair_ref[0:1, half:] = extra
+    pair_ref[1:2, half:] = jnp.zeros((1, LANES), f32)
+    pair = pair_ref[...].astype(bf16)
     for peer in range(out_ref.shape[0]):
-        out_ref[peer] = tile
-
-
-def to_step(got_ref, first_ref, count_ref, sq_norm_ref, keep_ref, share_ref, out_ref, grad_ref, tiles_ref):
-    groups, _, cap = tiles_ref.shape
+        out_ref[peer] = pair
+
+
+def to_step(groups, got_ref, count_ref, keep_ref, share_ref, out_ref, grad_ref):
     feats = got_ref.shape[0] // groups
-    start = first_ref.shape[2] - PEERS * cap
+    half = got_ref.shape[2] - LANES
+    cross, second_sq = 0.0, 0.0
     for s in range(groups):
-        for p in range(PEERS):
-            tiles_ref[s, p : p + 1, :] = first_ref[s, :, start + p * cap : start + (p + 1) * cap]
-    first_sq, cross, second_sq = 0.0, 0.0, 0.0
-    for s in range(groups):
-        first = tiles_ref[s]
-        second = got_ref[s].astype(f32)
-        for f in range(1, feats):
-            second = second + got_ref[f * groups + s].astype(f32)
-        first_sq = first_sq + first * first
-        cross = cross + first * second
-        second_sq = second_sq + second * second
-    first_sq, cross, second_sq = (
-        jnp.sum(row_sum(v), axis=0, keepdims=True) for v in (first_sq, cross, second_sq)
-    )
-    count, sq_norm, first_step = count_ref[:, :1], sq_norm_ref[:, :1], keep_ref[:, :1]
+        parts = [got_ref[f * groups + s].astype(f32) for f in range(feats)]
+        while len(parts) > 1:
+            parts = [a + b for a, b in zip(parts[::2], parts[1::2])]
+        cross = cross + parts[0][:, half:]
+        second_sq = second_sq + parts[0][:, :half] * parts[0][:, :half]
+    cross, second_sq = (jnp.sum(row_sum(v), axis=0, keepdims=True) for v in (cross, second_sq))
+    count, sq_norm = count_ref[:, :1], keep_ref[:, 2 * LANES : 2 * LANES + 1]
+    first_step, first_sq = keep_ref[:, :1], keep_ref[:, LANES : LANES + 1]
     sq_next = jnp.maximum(-first_step * cross / count, 0.0)
     beta = sq_next / sq_norm
     bend = jnp.maximum(second_sq + 2.0 * beta * cross + beta * beta * first_sq, 0.0)
@@ -210,7 +212,7 @@
     step = jnp.where(sq_next > 0.0, sq_next / jnp.where(sq_next > 0.0, below, 1.0), 0.0)
     grad_ref[...] = share_ref[...]
     direction = -share_ref[...]
-    out_ref[...] = first_step * direction + step * (keep_ref[:, LANES:] + beta * direction)
+    out_ref[...] = first_step * direction + step * (keep_ref[:, 3 * LANES :] + beta * direction)
 
 
 def exchange(values, axis):
@@ -264,38 +266,33 @@
         ),
     )
     got = exchange(part, "feat")
-    sq_norm, first = call(
-        to_image,
-        got,
-        curv,
-        rows,
-        out=(shape(1, LANES), shape(PEERS, 1, width + LANES + slots)),
-    )
-    first = exchange(first, "samp")
+    proj, part = call(
+        to_image, got, curv, rows, out=(shape(1, slots + LANES), shape(PEERS, 1, width + LANES))
+    )
+    got = exchange(part, "samp")
+    pair = (2, slots // 2 + LANES)
     keep, part = call(
         to_second,
-        first,
-        sq_norm,
+        got,
+        proj,
         curv,
         grad,
         count,
         rows,
         out=(
-            shape(1, LANES + share),
-            shape(lax.axis_size("feat") * samps, PEERS, cap, dtype=bf16),
+            shape(1, 3 * LANES + share),
+            shape(lax.axis_size("feat") * samps, *pair, dtype=bf16),
         ),
+        scratch=(pltpu.VMEM(pair, f32),),
     )
     got = exchange(part, ("feat", "samp"))
     return call(
-        to_step,
+        functools.partial(to_step, samps),
         got,
-        first,
         count,
-        sq_norm,
         keep,
         grad_share,
         out=(shape(1, share), shape(1, share)),
-        scratch=(pltpu.VMEM((samps, PEERS, cap), f32),),
     )
 
 

time: 102 us -> 102 us (level)
  no operation moved by 1% of the time
where the time goes in v7:
time: 102 us
  blocking collectives  97 us (95%)
  Pallas kernels  4.39 us (4%)
    all_to_all x6, blocking collectives, exchange(): return lax.all_to_all(values, axis, split_axis=0, concat_axis=0, tiled=True)  97 us
    pallas_call x7, Pallas kernels, call(): pl.pallas_call(kernel, out_shape=out, in_specs=[pl.BlockSpec(memory_space...  4.39 us

profile of v7, /device:TPU:1, one launch (start us, length us, event | category | flops | bytes accessed | tf_op | source)
XLA Modules:
  0.0 102.1 jit_solution(12800603129658344546)
XLA Ops:
  0.6 1.8 %pack_rows.1 = bf16[8,33,16,128]{3,2,1,0:T(8,128)(2,1)S(1)} custom-call(s32[1,512]{1,0:T(1,128)} %bitcast.2, s32[1,512]{1,0:T(1,128)} %bitcast.3, bf16[512,512]{1,0:T(8,128)(2,1)} %emb_in.1), custom_call_target="tpu_custom_call" | custom-call | tf_op jit(solution)/shard_map/pack_rows/pallas_call | solution.py:55
  2.5 0.0 copy-start
  2.5 38.4 %all_to_all.30.got_ref = bf16[8,33,16,128]{3,2,1,0:T(8,128)(2,1)S(1)} all-to-all(bf16[8,33,16,128]{3,2,1,0:T(8,128)(2,1)S(1)} %pack_rows.1), channel_id=1, replica_groups=mesh['plant'=8,'feat'=8,'samp'=8] {'plant'}, dimensions={0} | all-to-all | bytes 2162688 | tf_op jit(solution)/shard_map/all_to_all | solution.py:219
  40.9 0.0 copy-done
  40.9 0.4 take_rows.1
  41.3 11.5 %all_to_all.31.got_ref = f32[8,1,1024]{2,1,0:T(1,128)S(1)} all-to-all(f32[8,1,1024]{2,1,0:T(1,128)S(1)} %get-tuple-element.15), channel_id=1, replica_groups=mesh['plant'=8,'feat'=8,'samp'=8] {'feat'}, dimensions={0} | all-to-all | bytes 65536 | tf_op jit(solution)/shard_map/all_to_all | solution.py:219
  52.8 0.2 to_residual.1
  53.0 13.3 %all_to_all.32.got_ref = f32[8,1,640]{2,1,0:T(1,128)S(1)} all-to-all(f32[8,1,640]{2,1,0:T(1,128)S(1)} %get-tuple-element.18), channel_id=1, replica_groups=mesh['plant'=8,'feat'=8,'samp'=8] {'samp'}, dimensions={0} | all-to-all | bytes 40960 | tf_op jit(solution)/shard_map/all_to_all | solution.py:219
  66.3 0.4 to_direction.1
  66.7 9.3 %all_to_all.33.got_ref = f32[8,1,1152]{2,1,0:T(1,128)S(1)} all-to-all(f32[8,1,1152]{2,1,0:T(1,128)S(1)} %get-tuple-element.19), channel_id=1, replica_groups=mesh['plant'=8,'feat'=8,'samp'=8] {'feat'}, dimensions={0} | all-to-all | bytes 73728 | tf_op jit(solution)/shard_map/all_to_all | solution.py:219
  75.9 0.2 to_image.1
  76.2 9.0 %all_to_all.34.got_ref = f32[8,1,640]{2,1,0:T(1,128)S(1)} all-to-all(f32[8,1,640]{2,1,0:T(1,128)S(1)} %get-tuple-element.21), channel_id=1, replica_groups=mesh['plant'=8,'feat'=8,'samp'=8] {'samp'}, dimensions={0} | all-to-all | bytes 40960 | tf_op jit(solution)/shard_map/all_to_all | solution.py:219
  85.2 0.5 to_second.1
  85.7 15.6 %all_to_all.35.got_ref = bf16[64,2,640]{2,1,0:T(2,128)(2,1)S(1)} all-to-all(bf16[64,2,640]{2,1,0:T(2,128)(2,1)S(1)} %get-tuple-element.25), channel_id=1, replica_groups=mesh['plant'=8,'feat'=8,'samp'=8] {'feat','samp'}, dimensions={0} | all-to-all | bytes 327680 | tf_op jit(solution)/shard_map/all_to_all | solution.py:219
  101.3 0.7 to_step.1
Async XLA Ops:
  2.5 38.4 %copy-start = (f32[1,512]{1,0:T(1,128)S(1)}, f32[1,512]{1,0:T(1,128)}, u32[]{:S(2)}) copy-start(f32[1,512]{1,0:T(1,128)} %w_ref.3) | copy-start | bytes 6148

commit v8 on v7

--- a/solution.py
+++ b/solution.py
@@ -197,7 +197,7 @@
     half = got_ref.shape[2] - LANES
     cross, second_sq = 0.0, 0.0
     for s in range(groups):
-        parts = [got_ref[f * groups + s].astype(f32) for f in range(feats)]
+        parts = [got_ref[s * feats + f].astype(f32) for f in range(feats)]
         while len(parts) > 1:
             parts = [a + b for a, b in zip(parts[::2], parts[1::2])]
         cross = cross + parts[0][:, half:]
@@ -285,7 +285,7 @@
         ),
         scratch=(pltpu.VMEM(pair, f32),),
     )
-    got = exchange(part, ("feat", "samp"))
+    got = exchange(part, ("samp", "feat"))
     return call(
         functools.partial(to_step, samps),
         got,

time: 102 us -> 104 us (1.020)
  blocking collectives: 97 us -> 98.3 us
    all_to_all x6, blocking collectives: 97 us -> 98.3 us  [exchange(): return lax.all_to_all(values, axis, split_axis=0, concat_axis=0, tiled=True)]
where the time goes in v8:
time: 104 us; the launch traced here: 103 us
  blocking collectives  98.3 us (95%)
  Pallas kernels  4.39 us (4%)
    all_to_all x6, blocking collectives, exchange(): return lax.all_to_all(values, axis, split_axis=0, concat_axis=0, tiled=True)  98.3 us
    pallas_call x7, Pallas kernels, call(): pl.pallas_call(kernel, out_shape=out, in_specs=[pl.BlockSpec(memory_space...  4.39 us

profile of v8, /device:TPU:1, one launch (start us, length us, event | category | flops | bytes accessed | tf_op | source)
XLA Modules:
  0.0 103.3 jit_solution(7263256608308093100)
XLA Ops:
  0.6 1.8 %pack_rows.1 = bf16[8,33,16,128]{3,2,1,0:T(8,128)(2,1)S(1)} custom-call(s32[1,512]{1,0:T(1,128)} %bitcast.2, s32[1,512]{1,0:T(1,128)} %bitcast.3, bf16[512,512]{1,0:T(8,128)(2,1)} %emb_in.1), custom_call_target="tpu_custom_call" | custom-call | tf_op jit(solution)/shard_map/pack_rows/pallas_call | solution.py:55
  2.5 0.0 copy-start
  2.5 38.4 %all_to_all.30.got_ref = bf16[8,33,16,128]{3,2,1,0:T(8,128)(2,1)S(1)} all-to-all(bf16[8,33,16,128]{3,2,1,0:T(8,128)(2,1)S(1)} %pack_rows.1), channel_id=1, replica_groups=mesh['plant'=8,'feat'=8,'samp'=8] {'plant'}, dimensions={0} | all-to-all | bytes 2162688 | tf_op jit(solution)/shard_map/all_to_all | solution.py:219
  40.9 0.0 copy-done
  40.9 0.4 take_rows.1
  41.3 11.5 %all_to_all.31.got_ref = f32[8,1,1024]{2,1,0:T(1,128)S(1)} all-to-all(f32[8,1,1024]{2,1,0:T(1,128)S(1)} %get-tuple-element.15), channel_id=1, replica_groups=mesh['plant'=8,'feat'=8,'samp'=8] {'feat'}, dimensions={0} | all-to-all | bytes 65536 | tf_op jit(solution)/shard_map/all_to_all | solution.py:219
  52.8 0.2 to_residual.1
  53.0 13.3 %all_to_all.32.got_ref = f32[8,1,640]{2,1,0:T(1,128)S(1)} all-to-all(f32[8,1,640]{2,1,0:T(1,128)S(1)} %get-tuple-element.18), channel_id=1, replica_groups=mesh['plant'=8,'feat'=8,'samp'=8] {'samp'}, dimensions={0} | all-to-all | bytes 40960 | tf_op jit(solution)/shard_map/all_to_all | solution.py:219
  66.3 0.4 to_direction.1
  66.7 9.3 %all_to_all.33.got_ref = f32[8,1,1152]{2,1,0:T(1,128)S(1)} all-to-all(f32[8,1,1152]{2,1,0:T(1,128)S(1)} %get-tuple-element.19), channel_id=1, replica_groups=mesh['plant'=8,'feat'=8,'samp'=8] {'feat'}, dimensions={0} | all-to-all | bytes 73728 | tf_op jit(solution)/shard_map/all_to_all | solution.py:219
  75.9 0.2 to_image.1
  76.2 9.0 %all_to_all.34.got_ref = f32[8,1,640]{2,1,0:T(1,128)S(1)} all-to-all(f32[8,1,640]{2,1,0:T(1,128)S(1)} %get-tuple-element.21), channel_id=1, replica_groups=mesh['plant'=8,'feat'=8,'samp'=8] {'samp'}, dimensions={0} | all-to-all | bytes 40960 | tf_op jit(solution)/shard_map/all_to_all | solution.py:219
  85.2 0.5 to_second.1
  85.7 16.9 %all_to_all.35.got_ref = bf16[64,2,640]{2,1,0:T(2,128)(2,1)S(1)} all-to-all(bf16[64,2,640]{2,1,0:T(2,128)(2,1)S(1)} %get-tuple-element.25), channel_id=1, replica_groups=mesh['plant'=8,'feat'=8,'samp'=8] {'samp','feat'}, dimensions={0} | all-to-all | bytes 327680 | tf_op jit(solution)/shard_map/all_to_all | solution.py:219
  102.6 0.7 to_step.1
Async XLA Ops:
  2.5 38.4 %copy-start = (f32[1,512]{1,0:T(1,128)S(1)}, f32[1,512]{1,0:T(1,128)}, u32[]{:S(2)}) copy-start(f32[1,512]{1,0:T(1,128)} %w_ref.3) | copy-start | bytes 6148

commit v9 on v8

--- a/solution.py
+++ b/solution.py
@@ -197,7 +197,7 @@
     half = got_ref.shape[2] - LANES
     cross, second_sq = 0.0, 0.0
     for s in range(groups):
-        parts = [got_ref[s * feats + f].astype(f32) for f in range(feats)]
+        parts = [got_ref[(s - f) % groups * feats + f].astype(f32) for f in range(feats)]
         while len(parts) > 1:
             parts = [a + b for a, b in zip(parts[::2], parts[1::2])]
         cross = cross + parts[0][:, half:]
@@ -215,8 +215,10 @@
     out_ref[...] = first_step * direction + step * (keep_ref[:, 3 * LANES :] + beta * direction)
 
 
-def exchange(values, axis):
-    return lax.all_to_all(values, axis, split_axis=0, concat_axis=0, tiled=True)
+def exchange(values, axis, groups=None):
+    return lax.all_to_all(
+        values, axis, split_axis=0, concat_axis=0, tiled=True, axis_index_groups=groups
+    )
 
 
 def shards(embeddings, plant_ids, labels, weights):
@@ -285,7 +287,9 @@
         ),
         scratch=(pltpu.VMEM(pair, f32),),
     )
-    got = exchange(part, ("samp", "feat"))
+    feats = lax.axis_size("feat")
+    diagonals = [f * samps + (turn + f) % samps for turn in range(samps) for f in range(feats)]
+    got = exchange(part, ("feat", "samp"), [diagonals])
     return call(
         functools.partial(to_step, samps),
         got,

time: 104 us -> 103 us (level)
  no operation moved by 1% of the time
where the time goes in v9:
time: 103 us
  blocking collectives  98 us (95%)
  Pallas kernels  4.39 us (4%)
    all_to_all x6, blocking collectives, exchange(): lax.all_to_all(values, axis, split_axis=0, concat_axis=0, tiled=True, axi...  98 us
    pallas_call x7, Pallas kernels, call(): pl.pallas_call(kernel, out_shape=out, in_specs=[pl.BlockSpec(memory_space...  4.39 us

profile of v9, /device:TPU:1, one launch (start us, length us, event | category | flops | bytes accessed | tf_op | source)
XLA Modules:
  0.0 103.1 jit_solution(476693681724065800)
XLA Ops:
  0.6 1.8 %pack_rows.1 = bf16[8,33,16,128]{3,2,1,0:T(8,128)(2,1)S(1)} custom-call(s32[1,512]{1,0:T(1,128)} %bitcast.2, s32[1,512]{1,0:T(1,128)} %bitcast.3, bf16[512,512]{1,0:T(8,128)(2,1)} %emb_in.1), custom_call_target="tpu_custom_call" | custom-call | tf_op jit(solution)/shard_map/pack_rows/pallas_call | solution.py:55
  2.5 0.0 copy-start
  2.5 38.4 %all_to_all.30.got_ref = bf16[8,33,16,128]{3,2,1,0:T(8,128)(2,1)S(1)} all-to-all(bf16[8,33,16,128]{3,2,1,0:T(8,128)(2,1)S(1)} %pack_rows.1), channel_id=1, replica_groups=mesh['plant'=8,'feat'=8,'samp'=8] {'plant'}, dimensions={0} | all-to-all | bytes 2162688 | tf_op jit(solution)/shard_map/all_to_all | solution.py:219
  40.9 0.0 copy-done
  40.9 0.4 take_rows.1
  41.3 11.5 %all_to_all.31.got_ref = f32[8,1,1024]{2,1,0:T(1,128)S(1)} all-to-all(f32[8,1,1024]{2,1,0:T(1,128)S(1)} %get-tuple-element.15), channel_id=1, replica_groups=mesh['plant'=8,'feat'=8,'samp'=8] {'feat'}, dimensions={0} | all-to-all | bytes 65536 | tf_op jit(solution)/shard_map/all_to_all | solution.py:219
  52.8 0.2 to_residual.1
  53.0 13.3 %all_to_all.32.got_ref = f32[8,1,640]{2,1,0:T(1,128)S(1)} all-to-all(f32[8,1,640]{2,1,0:T(1,128)S(1)} %get-tuple-element.18), channel_id=1, replica_groups=mesh['plant'=8,'feat'=8,'samp'=8] {'samp'}, dimensions={0} | all-to-all | bytes 40960 | tf_op jit(solution)/shard_map/all_to_all | solution.py:219
  66.3 0.4 to_direction.1
  66.7 9.3 %all_to_all.33.got_ref = f32[8,1,1152]{2,1,0:T(1,128)S(1)} all-to-all(f32[8,1,1152]{2,1,0:T(1,128)S(1)} %get-tuple-element.19), channel_id=1, replica_groups=mesh['plant'=8,'feat'=8,'samp'=8] {'feat'}, dimensions={0} | all-to-all | bytes 73728 | tf_op jit(solution)/shard_map/all_to_all | solution.py:219
  75.9 0.2 to_image.1
  76.2 9.0 %all_to_all.34.got_ref = f32[8,1,640]{2,1,0:T(1,128)S(1)} all-to-all(f32[8,1,640]{2,1,0:T(1,128)S(1)} %get-tuple-element.21), channel_id=1, replica_groups=mesh['plant'=8,'feat'=8,'samp'=8] {'samp'}, dimensions={0} | all-to-all | bytes 40960 | tf_op jit(solution)/shard_map/all_to_all | solution.py:219
  85.2 0.5 to_second.1
  85.7 16.6 %all_to_all.35.got_ref = bf16[64,2,640]{2,1,0:T(2,128)(2,1)S(1)} all-to-all(bf16[64,2,640]{2,1,0:T(2,128)(2,1)S(1)} %get-tuple-element.25), channel_id=1, replica_groups={{0,9,18,27,36,45,54,63,1,10,19,28,37,46,55,56,2,11,20,29,38,47,48,57,3,..., dimensions={0} | all-to-all | bytes 327680 | tf_op jit(solution)/shard_map/all_to_all | solution.py:219
  102.3 0.7 to_step.1
Async XLA Ops:
  2.5 38.4 %copy-start = (f32[1,512]{1,0:T(1,128)S(1)}, f32[1,512]{1,0:T(1,128)}, u32[]{:S(2)}) copy-start(f32[1,512]{1,0:T(1,128)} %w_ref.3) | copy-start | bytes 6148

commit v10 on v9

--- a/solution.py
+++ b/solution.py
@@ -197,7 +197,7 @@
     half = got_ref.shape[2] - LANES
     cross, second_sq = 0.0, 0.0
     for s in range(groups):
-        parts = [got_ref[(s - f) % groups * feats + f].astype(f32) for f in range(feats)]
+        parts = [got_ref[f * groups + s].astype(f32) for f in range(feats)]
         while len(parts) > 1:
             parts = [a + b for a, b in zip(parts[::2], parts[1::2])]
         cross = cross + parts[0][:, half:]
@@ -288,8 +288,8 @@
         scratch=(pltpu.VMEM(pair, f32),),
     )
     feats = lax.axis_size("feat")
-    diagonals = [f * samps + (turn + f) % samps for turn in range(samps) for f in range(feats)]
-    got = exchange(part, ("feat", "samp"), [diagonals])
+    runs = [(f ^ 1) * samps + s for f in range(feats) for s in range(samps)]
+    got = exchange(part, ("feat", "samp"), [runs])
     return call(
         functools.partial(to_step, samps),
         got,

time: 103 us -> 103 us (level)
  no operation moved by 1% of the time
where the time goes in v10:
time: 103 us
  blocking collectives  97.5 us (95%)
  Pallas kernels  4.39 us (4%)
    all_to_all x6, blocking collectives, exchange(): lax.all_to_all(values, axis, split_axis=0, concat_axis=0, tiled=True, axi...  97.5 us
    pallas_call x7, Pallas kernels, call(): pl.pallas_call(kernel, out_shape=out, in_specs=[pl.BlockSpec(memory_space...  4.39 us

profile of v10, /device:TPU:1, one launch (start us, length us, event | category | flops | bytes accessed | tf_op | source)
XLA Modules:
  0.0 102.6 jit_solution(5689235176665507996)
XLA Ops:
  0.6 1.8 %pack_rows.1 = bf16[8,33,16,128]{3,2,1,0:T(8,128)(2,1)S(1)} custom-call(s32[1,512]{1,0:T(1,128)} %bitcast.2, s32[1,512]{1,0:T(1,128)} %bitcast.3, bf16[512,512]{1,0:T(8,128)(2,1)} %emb_in.1), custom_call_target="tpu_custom_call" | custom-call | tf_op jit(solution)/shard_map/pack_rows/pallas_call | solution.py:55
  2.5 0.0 copy-start
  2.5 38.4 %all_to_all.30.got_ref = bf16[8,33,16,128]{3,2,1,0:T(8,128)(2,1)S(1)} all-to-all(bf16[8,33,16,128]{3,2,1,0:T(8,128)(2,1)S(1)} %pack_rows.1), channel_id=1, replica_groups=mesh['plant'=8,'feat'=8,'samp'=8] {'plant'}, dimensions={0} | all-to-all | bytes 2162688 | tf_op jit(solution)/shard_map/all_to_all | solution.py:219
  40.9 0.0 copy-done
  40.9 0.4 take_rows.1
  41.3 11.5 %all_to_all.31.got_ref = f32[8,1,1024]{2,1,0:T(1,128)S(1)} all-to-all(f32[8,1,1024]{2,1,0:T(1,128)S(1)} %get-tuple-element.15), channel_id=1, replica_groups=mesh['plant'=8,'feat'=8,'samp'=8] {'feat'}, dimensions={0} | all-to-all | bytes 65536 | tf_op jit(solution)/shard_map/all_to_all | solution.py:219
  52.8 0.2 to_residual.1
  53.0 13.3 %all_to_all.32.got_ref = f32[8,1,640]{2,1,0:T(1,128)S(1)} all-to-all(f32[8,1,640]{2,1,0:T(1,128)S(1)} %get-tuple-element.18), channel_id=1, replica_groups=mesh['plant'=8,'feat'=8,'samp'=8] {'samp'}, dimensions={0} | all-to-all | bytes 40960 | tf_op jit(solution)/shard_map/all_to_all | solution.py:219
  66.3 0.4 to_direction.1
  66.7 9.3 %all_to_all.33.got_ref = f32[8,1,1152]{2,1,0:T(1,128)S(1)} all-to-all(f32[8,1,1152]{2,1,0:T(1,128)S(1)} %get-tuple-element.19), channel_id=1, replica_groups=mesh['plant'=8,'feat'=8,'samp'=8] {'feat'}, dimensions={0} | all-to-all | bytes 73728 | tf_op jit(solution)/shard_map/all_to_all | solution.py:219
  75.9 0.2 to_image.1
  76.2 9.0 %all_to_all.34.got_ref = f32[8,1,640]{2,1,0:T(1,128)S(1)} all-to-all(f32[8,1,640]{2,1,0:T(1,128)S(1)} %get-tuple-element.21), channel_id=1, replica_groups=mesh['plant'=8,'feat'=8,'samp'=8] {'samp'}, dimensions={0} | all-to-all | bytes 40960 | tf_op jit(solution)/shard_map/all_to_all | solution.py:219
  85.2 0.5 to_second.1
  85.7 16.1 %all_to_all.35.got_ref = bf16[64,2,640]{2,1,0:T(2,128)(2,1)S(1)} all-to-all(bf16[64,2,640]{2,1,0:T(2,128)(2,1)S(1)} %get-tuple-element.25), channel_id=1, replica_groups={{8,9,10,11,12,13,14,15,0,1,2,3,4,5,6,7,24,25,26,27,28,29,30,31,16,17,18..., dimensions={0} | all-to-all | bytes 327680 | tf_op jit(solution)/shard_map/all_to_all | solution.py:219
  101.9 0.7 to_step.1
Async XLA Ops:
  2.5 38.4 %copy-start = (f32[1,512]{1,0:T(1,128)S(1)}, f32[1,512]{1,0:T(1,128)}, u32[]{:S(2)}) copy-start(f32[1,512]{1,0:T(1,128)} %w_ref.3) | copy-start | bytes 6148

commit v11 on v10

--- a/solution.py
+++ b/solution.py
@@ -197,7 +197,7 @@
     half = got_ref.shape[2] - LANES
     cross, second_sq = 0.0, 0.0
     for s in range(groups):
-        parts = [got_ref[f * groups + s].astype(f32) for f in range(feats)]
+        parts = [got_ref[run * groups + s].astype(f32) for run in range(feats)]
         while len(parts) > 1:
             parts = [a + b for a, b in zip(parts[::2], parts[1::2])]
         cross = cross + parts[0][:, half:]
@@ -288,7 +288,7 @@
         scratch=(pltpu.VMEM(pair, f32),),
     )
     feats = lax.axis_size("feat")
-    runs = [(f ^ 1) * samps + s for f in range(feats) for s in range(samps)]
+    runs = [f * samps + s for core in (0, 1) for f in range(core, feats, 2) for s in range(samps)]
     got = exchange(part, ("feat", "samp"), [runs])
     return call(
         functools.partial(to_step, samps),

time: 103 us -> 103 us (level)
  no operation moved by 1% of the time
where the time goes in v11:
time: 103 us
  blocking collectives  98.1 us (95%)
  Pallas kernels  4.39 us (4%)
    all_to_all x6, blocking collectives, exchange(): lax.all_to_all(values, axis, split_axis=0, concat_axis=0, tiled=True, axi...  98.1 us
    pallas_call x7, Pallas kernels, call(): pl.pallas_call(kernel, out_shape=out, in_specs=[pl.BlockSpec(memory_space...  4.39 us

profile of v11, /device:TPU:1, one launch (start us, length us, event | category | flops | bytes accessed | tf_op | source)
XLA Modules:
  0.0 103.1 jit_solution(6323968201299694734)
XLA Ops:
  0.6 1.8 %pack_rows.1 = bf16[8,33,16,128]{3,2,1,0:T(8,128)(2,1)S(1)} custom-call(s32[1,512]{1,0:T(1,128)} %bitcast.2, s32[1,512]{1,0:T(1,128)} %bitcast.3, bf16[512,512]{1,0:T(8,128)(2,1)} %emb_in.1), custom_call_target="tpu_custom_call" | custom-call | tf_op jit(solution)/shard_map/pack_rows/pallas_call | solution.py:55
  2.5 0.0 copy-start
  2.5 38.4 %all_to_all.30.got_ref = bf16[8,33,16,128]{3,2,1,0:T(8,128)(2,1)S(1)} all-to-all(bf16[8,33,16,128]{3,2,1,0:T(8,128)(2,1)S(1)} %pack_rows.1), channel_id=1, replica_groups=mesh['plant'=8,'feat'=8,'samp'=8] {'plant'}, dimensions={0} | all-to-all | bytes 2162688 | tf_op jit(solution)/shard_map/all_to_all | solution.py:219
  40.9 0.0 copy-done
  40.9 0.4 take_rows.1
  41.3 11.5 %all_to_all.31.got_ref = f32[8,1,1024]{2,1,0:T(1,128)S(1)} all-to-all(f32[8,1,1024]{2,1,0:T(1,128)S(1)} %get-tuple-element.15), channel_id=1, replica_groups=mesh['plant'=8,'feat'=8,'samp'=8] {'feat'}, dimensions={0} | all-to-all | bytes 65536 | tf_op jit(solution)/shard_map/all_to_all | solution.py:219
  52.8 0.2 to_residual.1
  53.0 13.3 %all_to_all.32.got_ref = f32[8,1,640]{2,1,0:T(1,128)S(1)} all-to-all(f32[8,1,640]{2,1,0:T(1,128)S(1)} %get-tuple-element.18), channel_id=1, replica_groups=mesh['plant'=8,'feat'=8,'samp'=8] {'samp'}, dimensions={0} | all-to-all | bytes 40960 | tf_op jit(solution)/shard_map/all_to_all | solution.py:219
  66.3 0.4 to_direction.1
  66.7 9.3 %all_to_all.33.got_ref = f32[8,1,1152]{2,1,0:T(1,128)S(1)} all-to-all(f32[8,1,1152]{2,1,0:T(1,128)S(1)} %get-tuple-element.19), channel_id=1, replica_groups=mesh['plant'=8,'feat'=8,'samp'=8] {'feat'}, dimensions={0} | all-to-all | bytes 73728 | tf_op jit(solution)/shard_map/all_to_all | solution.py:219
  75.9 0.2 to_image.1
  76.2 9.0 %all_to_all.34.got_ref = f32[8,1,640]{2,1,0:T(1,128)S(1)} all-to-all(f32[8,1,640]{2,1,0:T(1,128)S(1)} %get-tuple-element.21), channel_id=1, replica_groups=mesh['plant'=8,'feat'=8,'samp'=8] {'samp'}, dimensions={0} | all-to-all | bytes 40960 | tf_op jit(solution)/shard_map/all_to_all | solution.py:219
  85.2 0.5 to_second.1
  85.7 16.7 %all_to_all.35.got_ref = bf16[64,2,640]{2,1,0:T(2,128)(2,1)S(1)} all-to-all(bf16[64,2,640]{2,1,0:T(2,128)(2,1)S(1)} %get-tuple-element.25), channel_id=1, replica_groups={{0,1,2,3,4,5,6,7,16,17,18,19,20,21,22,23,32,33,34,35,36,37,38,39,48,49,..., dimensions={0} | all-to-all | bytes 327680 | tf_op jit(solution)/shard_map/all_to_all | solution.py:219
  102.4 0.7 to_step.1
Async XLA Ops:
  2.5 38.4 %copy-start = (f32[1,512]{1,0:T(1,128)S(1)}, f32[1,512]{1,0:T(1,128)}, u32[]{:S(2)}) copy-start(f32[1,512]{1,0:T(1,128)} %w_ref.3) | copy-start | bytes 6148

commit v12 on v11

--- a/solution.py
+++ b/solution.py
@@ -288,7 +288,12 @@
         scratch=(pltpu.VMEM(pair, f32),),
     )
     feats = lax.axis_size("feat")
-    runs = [f * samps + s for core in (0, 1) for f in range(core, feats, 2) for s in range(samps)]
+    runs = [
+        (f + core) * samps + s
+        for f in range(feats - 2, -1, -2)
+        for core in (0, 1)
+        for s in range(samps)
+    ]
     got = exchange(part, ("feat", "samp"), [runs])
     return call(
         functools.partial(to_step, samps),

time: 103 us -> 103 us (level)
  no operation moved by 1% of the time
where the time goes in v12:
time: 103 us; the launch traced here: 102 us
  blocking collectives  97.3 us (94%)
  Pallas kernels  4.39 us (4%)
    all_to_all x6, blocking collectives, exchange(): lax.all_to_all(values, axis, split_axis=0, concat_axis=0, tiled=True, axi...  97.3 us
    pallas_call x7, Pallas kernels, call(): pl.pallas_call(kernel, out_shape=out, in_specs=[pl.BlockSpec(memory_space...  4.39 us

profile of v12, /device:TPU:1, one launch (start us, length us, event | category | flops | bytes accessed | tf_op | source)
XLA Modules:
  0.0 102.4 jit_solution(8656991334306129627)
XLA Ops:
  0.6 1.8 %pack_rows.1 = bf16[8,33,16,128]{3,2,1,0:T(8,128)(2,1)S(1)} custom-call(s32[1,512]{1,0:T(1,128)} %bitcast.2, s32[1,512]{1,0:T(1,128)} %bitcast.3, bf16[512,512]{1,0:T(8,128)(2,1)} %emb_in.1), custom_call_target="tpu_custom_call" | custom-call | tf_op jit(solution)/shard_map/pack_rows/pallas_call | solution.py:55
  2.5 0.0 copy-start
  2.5 38.4 %all_to_all.30.got_ref = bf16[8,33,16,128]{3,2,1,0:T(8,128)(2,1)S(1)} all-to-all(bf16[8,33,16,128]{3,2,1,0:T(8,128)(2,1)S(1)} %pack_rows.1), channel_id=1, replica_groups=mesh['plant'=8,'feat'=8,'samp'=8] {'plant'}, dimensions={0} | all-to-all | bytes 2162688 | tf_op jit(solution)/shard_map/all_to_all | solution.py:219
  40.9 0.0 copy-done
  40.9 0.4 take_rows.1
  41.3 11.5 %all_to_all.31.got_ref = f32[8,1,1024]{2,1,0:T(1,128)S(1)} all-to-all(f32[8,1,1024]{2,1,0:T(1,128)S(1)} %get-tuple-element.15), channel_id=1, replica_groups=mesh['plant'=8,'feat'=8,'samp'=8] {'feat'}, dimensions={0} | all-to-all | bytes 65536 | tf_op jit(solution)/shard_map/all_to_all | solution.py:219
  52.8 0.2 to_residual.1
  53.0 13.3 %all_to_all.32.got_ref = f32[8,1,640]{2,1,0:T(1,128)S(1)} all-to-all(f32[8,1,640]{2,1,0:T(1,128)S(1)} %get-tuple-element.18), channel_id=1, replica_groups=mesh['plant'=8,'feat'=8,'samp'=8] {'samp'}, dimensions={0} | all-to-all | bytes 40960 | tf_op jit(solution)/shard_map/all_to_all | solution.py:219
  66.3 0.4 to_direction.1
  66.7 9.3 %all_to_all.33.got_ref = f32[8,1,1152]{2,1,0:T(1,128)S(1)} all-to-all(f32[8,1,1152]{2,1,0:T(1,128)S(1)} %get-tuple-element.19), channel_id=1, replica_groups=mesh['plant'=8,'feat'=8,'samp'=8] {'feat'}, dimensions={0} | all-to-all | bytes 73728 | tf_op jit(solution)/shard_map/all_to_all | solution.py:219
  75.9 0.2 to_image.1
  76.2 9.0 %all_to_all.34.got_ref = f32[8,1,640]{2,1,0:T(1,128)S(1)} all-to-all(f32[8,1,640]{2,1,0:T(1,128)S(1)} %get-tuple-element.21), channel_id=1, replica_groups=mesh['plant'=8,'feat'=8,'samp'=8] {'samp'}, dimensions={0} | all-to-all | bytes 40960 | tf_op jit(solution)/shard_map/all_to_all | solution.py:219
  85.2 0.5 to_second.1
  85.7 15.9 %all_to_all.35.got_ref = bf16[64,2,640]{2,1,0:T(2,128)(2,1)S(1)} all-to-all(bf16[64,2,640]{2,1,0:T(2,128)(2,1)S(1)} %get-tuple-element.25), channel_id=1, replica_groups={{48,49,50,51,52,53,54,55,56,57,58,59,60,61,62,63,32,33,34,35,36,37,38,3..., dimensions={0} | all-to-all | bytes 327680 | tf_op jit(solution)/shard_map/all_to_all | solution.py:219
  101.6 0.7 to_step.1
Async XLA Ops:
  2.5 38.4 %copy-start = (f32[1,512]{1,0:T(1,128)S(1)}, f32[1,512]{1,0:T(1,128)}, u32[]{:S(2)}) copy-start(f32[1,512]{1,0:T(1,128)} %w_ref.3) | copy-start | bytes 6148

commit v13 on v6

--- a/solution.py
+++ b/solution.py
@@ -9,6 +9,7 @@
 
 penalty = 0.1
 PEERS = 8
+SPREAD = (0, 4, 2, 6, 1, 5, 3, 7)
 LANES = 128
 DEEP = 16
 GRANT = 12 << 20
@@ -94,15 +95,15 @@
     copies[2].wait()
     emb = emb_ref[...]
     across = emb.shape[1] // LANES
-    for p in range(PEERS):
+    for at, p in enumerate(SPREAD):
         pick = (at_rank & (ids == p)).astype(f32).astype(bf16)
         picked = nn(pick, emb).astype(bf16)
         for down in range(cap // DEEP):
             for over in range(across):
-                out_ref[p, down * across + over] = picked[
+                out_ref[at, down * across + over] = picked[
                     down * DEEP : (down + 1) * DEEP, over * LANES : (over + 1) * LANES
                 ]
-        out_ref[p, cap // DEEP * across] = jnp.broadcast_to(
+        out_ref[at, cap // DEEP * across] = jnp.broadcast_to(
             tag_slots[p : p + 1], (DEEP, cap)
         ).astype(bf16)
 
@@ -213,8 +214,10 @@
     out_ref[...] = first_step * direction + step * (keep_ref[:, LANES:] + beta * direction)
 
 
-def exchange(values, axis):
-    return lax.all_to_all(values, axis, split_axis=0, concat_axis=0, tiled=True)
+def exchange(values, axis, groups=None):
+    return lax.all_to_all(
+        values, axis, split_axis=0, concat_axis=0, tiled=True, axis_index_groups=groups
+    )
 
 
 def shards(embeddings, plant_ids, labels, weights):
@@ -239,7 +242,7 @@
         ),
         space=pltpu.HBM,
     )
-    got = exchange(sent, "plant")
+    got = exchange(sent, "plant", [list(SPREAD)])
     rows, tags, part = call(
         functools.partial(take_rows, cap),
         got,

time: 102 us -> 102 us (level)
  no operation moved by 1% of the time
where the time goes in v13:
time: 102 us; the launch traced here: 101 us
  blocking collectives  96.4 us (95%)
  Pallas kernels  4.27 us (4%)
    all_to_all x6, blocking collectives, exchange(): lax.all_to_all(values, axis, split_axis=0, concat_axis=0, tiled=True, axi...  96.4 us
    pallas_call x7, Pallas kernels, call(): pl.pallas_call(kernel, out_shape=out, in_specs=[pl.BlockSpec(memory_space...  4.27 us

profile of v13, /device:TPU:1, one launch (start us, length us, event | category | flops | bytes accessed | tf_op | source)
XLA Modules:
  0.0 101.3 jit_solution(4634238397341379932)
XLA Ops:
  0.6 1.8 %pack_rows.1 = bf16[8,33,16,128]{3,2,1,0:T(8,128)(2,1)S(1)} custom-call(s32[1,512]{1,0:T(1,128)} %bitcast.2, s32[1,512]{1,0:T(1,128)} %bitcast.3, bf16[512,512]{1,0:T(8,128)(2,1)} %emb_in.1), custom_call_target="tpu_custom_call" | custom-call | tf_op jit(solution)/shard_map/pack_rows/pallas_call | solution.py:56
  2.5 0.0 copy-start
  2.5 38.1 %all_to_all.30.got_ref = bf16[8,33,16,128]{3,2,1,0:T(8,128)(2,1)S(1)} all-to-all(bf16[8,33,16,128]{3,2,1,0:T(8,128)(2,1)S(1)} %pack_rows.1), channel_id=1, replica_groups={{0,256,128,384,64,320,192,448},{1,257,129,385,65,321,193,449},{2,258,13..., dimensions={0} | all-to-all | bytes 2162688 | tf_op jit(solution)/shard_map/all_to_all | solution.py:218
  40.6 0.0 copy-done
  40.6 0.4 take_rows.1
  41.0 11.0 %all_to_all.31.got_ref = f32[8,1,1024]{2,1,0:T(1,128)S(1)} all-to-all(f32[8,1,1024]{2,1,0:T(1,128)S(1)} %get-tuple-element.15), channel_id=1, replica_groups=mesh['plant'=8,'feat'=8,'samp'=8] {'feat'}, dimensions={0} | all-to-all | bytes 65536 | tf_op jit(solution)/shard_map/all_to_all | solution.py:218
  52.1 0.2 to_residual.1
  52.3 13.3 %all_to_all.32.got_ref = f32[8,1,640]{2,1,0:T(1,128)S(1)} all-to-all(f32[8,1,640]{2,1,0:T(1,128)S(1)} %get-tuple-element.18), channel_id=1, replica_groups=mesh['plant'=8,'feat'=8,'samp'=8] {'samp'}, dimensions={0} | all-to-all | bytes 40960 | tf_op jit(solution)/shard_map/all_to_all | solution.py:218
  65.6 0.4 to_direction.1
  66.0 9.3 %all_to_all.33.got_ref = f32[8,1,1152]{2,1,0:T(1,128)S(1)} all-to-all(f32[8,1,1152]{2,1,0:T(1,128)S(1)} %get-tuple-element.19), channel_id=1, replica_groups=mesh['plant'=8,'feat'=8,'samp'=8] {'feat'}, dimensions={0} | all-to-all | bytes 73728 | tf_op jit(solution)/shard_map/all_to_all | solution.py:218
  75.2 0.2 to_image.1
  75.5 9.5 %all_to_all.34.got_ref.first_ref = f32[8,1,1664]{2,1,0:T(1,128)S(1)} all-to-all(f32[8,1,1664]{2,1,0:T(1,128)S(1)} %get-tuple-element.21), channel_id=1, replica_groups=mesh['plant'=8,'feat'=8,'samp'=8] {'samp'}, dimensions={0} | all-to-all | bytes 106496 | tf_op jit(solution)/shard_map/all_to_all | solution.py:218
  85.0 0.4 to_second.1
  85.5 15.1 %all_to_all.35.got_ref = bf16[64,8,128]{2,1,0:T(8,128)(2,1)S(1)} all-to-all(bf16[64,8,128]{2,1,0:T(8,128)(2,1)S(1)} %get-tuple-element.25), channel_id=1, replica_groups=mesh['plant'=8,'feat'=8,'samp'=8] {'feat','samp'}, dimensions={0} | all-to-all | bytes 262144 | tf_op jit(solution)/shard_map/all_to_all | solution.py:218
  100.6 0.7 to_step.1
Async XLA Ops:
  2.5 38.1 %copy-start = (f32[1,512]{1,0:T(1,128)S(1)}, f32[1,512]{1,0:T(1,128)}, u32[]{:S(2)}) copy-start(f32[1,512]{1,0:T(1,128)} %w_ref.3) | copy-start | bytes 6148

commit v14 on v6

--- a/solution.py
+++ b/solution.py
@@ -9,6 +9,7 @@
 
 penalty = 0.1
 PEERS = 8
+SPREAD = (0, 4, 2, 6, 1, 5, 3, 7)
 LANES = 128
 DEEP = 16
 GRANT = 12 << 20
@@ -191,8 +192,8 @@
         for p in range(PEERS):
             tiles_ref[s, p : p + 1, :] = first_ref[s, :, start + p * cap : start + (p + 1) * cap]
     first_sq, cross, second_sq = 0.0, 0.0, 0.0
-    for s in range(groups):
-        first = tiles_ref[s]
+    for at, s in enumerate(SPREAD):
+        first = tiles_ref[at]
         second = got_ref[s].astype(f32)
         for f in range(1, feats):
             second = second + got_ref[f * groups + s].astype(f32)
@@ -213,8 +214,10 @@
     out_ref[...] = first_step * direction + step * (keep_ref[:, LANES:] + beta * direction)
 
 
-def exchange(values, axis):
-    return lax.all_to_all(values, axis, split_axis=0, concat_axis=0, tiled=True)
+def exchange(values, axis, groups=None):
+    return lax.all_to_all(
+        values, axis, split_axis=0, concat_axis=0, tiled=True, axis_index_groups=groups
+    )
 
 
 def shards(embeddings, plant_ids, labels, weights):
@@ -250,7 +253,7 @@
     curv, part = call(
         to_residual, got, tags, rows, out=(shape(1, slots), shape(PEERS, 1, width + LANES))
     )
-    got = exchange(part, "samp")
+    got = exchange(part, "samp", [list(SPREAD)])
     grad, count, grad_share, part = call(
         to_direction,
         got,
@@ -271,7 +274,7 @@
         rows,
         out=(shape(1, LANES), shape(PEERS, 1, width + LANES + slots)),
     )
-    first = exchange(first, "samp")
+    first = exchange(first, "samp", [list(SPREAD)])
     keep, part = call(
         to_second,
         first,

time: 102 us -> 102 us (level)
  no operation moved by 1% of the time
where the time goes in v14:
time: 102 us; the launch traced here: 101 us
  blocking collectives  96.5 us (95%)
  Pallas kernels  4.26 us (4%)
    all_to_all x6, blocking collectives, exchange(): lax.all_to_all(values, axis, split_axis=0, concat_axis=0, tiled=True, axi...  96.5 us
    pallas_call x7, Pallas kernels, call(): pl.pallas_call(kernel, out_shape=out, in_specs=[pl.BlockSpec(memory_space...  4.26 us

profile of v14, /device:TPU:1, one launch (start us, length us, event | category | flops | bytes accessed | tf_op | source)
XLA Modules:
  0.0 101.4 jit_solution(16864189877005114092)
XLA Ops:
  0.6 1.8 %pack_rows.1 = bf16[8,33,16,128]{3,2,1,0:T(8,128)(2,1)S(1)} custom-call(s32[1,512]{1,0:T(1,128)} %bitcast.2, s32[1,512]{1,0:T(1,128)} %bitcast.3, bf16[512,512]{1,0:T(8,128)(2,1)} %emb_in.1), custom_call_target="tpu_custom_call" | custom-call | tf_op jit(solution)/shard_map/pack_rows/pallas_call | solution.py:56
  2.5 0.0 copy-start
  2.5 38.4 %all_to_all.30.got_ref = bf16[8,33,16,128]{3,2,1,0:T(8,128)(2,1)S(1)} all-to-all(bf16[8,33,16,128]{3,2,1,0:T(8,128)(2,1)S(1)} %pack_rows.1), channel_id=1, replica_groups=mesh['plant'=8,'feat'=8,'samp'=8] {'plant'}, dimensions={0} | all-to-all | bytes 2162688 | tf_op jit(solution)/shard_map/all_to_all | solution.py:218
  40.9 0.0 copy-done
  40.9 0.4 take_rows.1
  41.3 11.5 %all_to_all.31.got_ref = f32[8,1,1024]{2,1,0:T(1,128)S(1)} all-to-all(f32[8,1,1024]{2,1,0:T(1,128)S(1)} %get-tuple-element.15), channel_id=1, replica_groups=mesh['plant'=8,'feat'=8,'samp'=8] {'feat'}, dimensions={0} | all-to-all | bytes 65536 | tf_op jit(solution)/shard_map/all_to_all | solution.py:218
  52.8 0.2 to_residual.1
  53.0 13.2 %all_to_all.32.got_ref = f32[8,1,640]{2,1,0:T(1,128)S(1)} all-to-all(f32[8,1,640]{2,1,0:T(1,128)S(1)} %get-tuple-element.18), channel_id=1, replica_groups={{0,4,2,6,1,5,3,7},{8,12,10,14,9,13,11,15},{16,20,18,22,17,21,19,23},{24..., dimensions={0} | all-to-all | bytes 40960 | tf_op jit(solution)/shard_map/all_to_all | solution.py:218
  66.2 0.4 to_direction.1
  66.6 9.3 %all_to_all.33.got_ref = f32[8,1,1152]{2,1,0:T(1,128)S(1)} all-to-all(f32[8,1,1152]{2,1,0:T(1,128)S(1)} %get-tuple-element.19), channel_id=1, replica_groups=mesh['plant'=8,'feat'=8,'samp'=8] {'feat'}, dimensions={0} | all-to-all | bytes 73728 | tf_op jit(solution)/shard_map/all_to_all | solution.py:218
  75.8 0.2 to_image.1
  76.1 9.0 %all_to_all.34.got_ref.first_ref = f32[8,1,1664]{2,1,0:T(1,128)S(1)} all-to-all(f32[8,1,1664]{2,1,0:T(1,128)S(1)} %get-tuple-element.21), channel_id=1, replica_groups={{0,4,2,6,1,5,3,7},{8,12,10,14,9,13,11,15},{16,20,18,22,17,21,19,23},{24..., dimensions={0} | all-to-all | bytes 106496 | tf_op jit(solution)/shard_map/all_to_all | solution.py:218
  85.1 0.4 to_second.1
  85.5 15.2 %all_to_all.35.got_ref = bf16[64,8,128]{2,1,0:T(8,128)(2,1)S(1)} all-to-all(bf16[64,8,128]{2,1,0:T(8,128)(2,1)S(1)} %get-tuple-element.25), channel_id=1, replica_groups=mesh['plant'=8,'feat'=8,'samp'=8] {'feat','samp'}, dimensions={0} | all-to-all | bytes 262144 | tf_op jit(solution)/shard_map/all_to_all | solution.py:218
  100.7 0.7 to_step.1
Async XLA Ops:
  2.5 38.4 %copy-start = (f32[1,512]{1,0:T(1,128)S(1)}, f32[1,512]{1,0:T(1,128)}, u32[]{:S(2)}) copy-start(f32[1,512]{1,0:T(1,128)} %w_ref.3) | copy-start | bytes 6148

commit v15 on v14

--- a/solution.py
+++ b/solution.py
@@ -95,15 +95,15 @@
     copies[2].wait()
     emb = emb_ref[...]
     across = emb.shape[1] // LANES
-    for p in range(PEERS):
+    for at, p in enumerate(SPREAD):
         pick = (at_rank & (ids == p)).astype(f32).astype(bf16)
         picked = nn(pick, emb).astype(bf16)
         for down in range(cap // DEEP):
             for over in range(across):
-                out_ref[p, down * across + over] = picked[
+                out_ref[at, down * across + over] = picked[
                     down * DEEP : (down + 1) * DEEP, over * LANES : (over + 1) * LANES
                 ]
-        out_ref[p, cap // DEEP * across] = jnp.broadcast_to(
+        out_ref[at, cap // DEEP * across] = jnp.broadcast_to(
             tag_slots[p : p + 1], (DEEP, cap)
         ).astype(bf16)
 
@@ -242,7 +242,7 @@
         ),
         space=pltpu.HBM,
     )
-    got = exchange(sent, "plant")
+    got = exchange(sent, "plant", [list(SPREAD)])
     rows, tags, part = call(
         functools.partial(take_rows, cap),
         got,

time: 102 us -> 101 us (level)
  no operation moved by 1% of the time
where the time goes in v15:
time: 101 us
  blocking collectives  95.8 us (95%)
  Pallas kernels  4.26 us (4%)
    all_to_all x6, blocking collectives, exchange(): lax.all_to_all(values, axis, split_axis=0, concat_axis=0, tiled=True, axi...  95.8 us
    pallas_call x7, Pallas kernels, call(): pl.pallas_call(kernel, out_shape=out, in_specs=[pl.BlockSpec(memory_space...  4.26 us

profile of v15, /device:TPU:1, one launch (start us, length us, event | category | flops | bytes accessed | tf_op | source)
XLA Modules:
  0.0 100.7 jit_solution(7136894511251152784)
XLA Ops:
  0.6 1.8 %pack_rows.1 = bf16[8,33,16,128]{3,2,1,0:T(8,128)(2,1)S(1)} custom-call(s32[1,512]{1,0:T(1,128)} %bitcast.2, s32[1,512]{1,0:T(1,128)} %bitcast.3, bf16[512,512]{1,0:T(8,128)(2,1)} %emb_in.1), custom_call_target="tpu_custom_call" | custom-call | tf_op jit(solution)/shard_map/pack_rows/pallas_call | solution.py:56
  2.5 0.0 copy-start
  2.5 38.1 %all_to_all.30.got_ref = bf16[8,33,16,128]{3,2,1,0:T(8,128)(2,1)S(1)} all-to-all(bf16[8,33,16,128]{3,2,1,0:T(8,128)(2,1)S(1)} %pack_rows.1), channel_id=1, replica_groups={{0,256,128,384,64,320,192,448},{1,257,129,385,65,321,193,449},{2,258,13..., dimensions={0} | all-to-all | bytes 2162688 | tf_op jit(solution)/shard_map/all_to_all | solution.py:218
  40.6 0.0 copy-done
  40.6 0.4 take_rows.1
  41.0 11.0 %all_to_all.31.got_ref = f32[8,1,1024]{2,1,0:T(1,128)S(1)} all-to-all(f32[8,1,1024]{2,1,0:T(1,128)S(1)} %get-tuple-element.15), channel_id=1, replica_groups=mesh['plant'=8,'feat'=8,'samp'=8] {'feat'}, dimensions={0} | all-to-all | bytes 65536 | tf_op jit(solution)/shard_map/all_to_all | solution.py:218
  52.1 0.2 to_residual.1
  52.3 13.2 %all_to_all.32.got_ref = f32[8,1,640]{2,1,0:T(1,128)S(1)} all-to-all(f32[8,1,640]{2,1,0:T(1,128)S(1)} %get-tuple-element.18), channel_id=1, replica_groups={{0,4,2,6,1,5,3,7},{8,12,10,14,9,13,11,15},{16,20,18,22,17,21,19,23},{24..., dimensions={0} | all-to-all | bytes 40960 | tf_op jit(solution)/shard_map/all_to_all | solution.py:218
  65.5 0.4 to_direction.1
  65.9 9.3 %all_to_all.33.got_ref = f32[8,1,1152]{2,1,0:T(1,128)S(1)} all-to-all(f32[8,1,1152]{2,1,0:T(1,128)S(1)} %get-tuple-element.19), channel_id=1, replica_groups=mesh['plant'=8,'feat'=8,'samp'=8] {'feat'}, dimensions={0} | all-to-all | bytes 73728 | tf_op jit(solution)/shard_map/all_to_all | solution.py:218
  75.1 0.2 to_image.1
  75.4 9.0 %all_to_all.34.got_ref.first_ref = f32[8,1,1664]{2,1,0:T(1,128)S(1)} all-to-all(f32[8,1,1664]{2,1,0:T(1,128)S(1)} %get-tuple-element.21), channel_id=1, replica_groups={{0,4,2,6,1,5,3,7},{8,12,10,14,9,13,11,15},{16,20,18,22,17,21,19,23},{24..., dimensions={0} | all-to-all | bytes 106496 | tf_op jit(solution)/shard_map/all_to_all | solution.py:218
  84.3 0.4 to_second.1
  84.8 15.2 %all_to_all.35.got_ref = bf16[64,8,128]{2,1,0:T(8,128)(2,1)S(1)} all-to-all(bf16[64,8,128]{2,1,0:T(8,128)(2,1)S(1)} %get-tuple-element.25), channel_id=1, replica_groups=mesh['plant'=8,'feat'=8,'samp'=8] {'feat','samp'}, dimensions={0} | all-to-all | bytes 262144 | tf_op jit(solution)/shard_map/all_to_all | solution.py:218
  100.0 0.7 to_step.1
Async XLA Ops:
  2.5 38.1 %copy-start = (f32[1,512]{1,0:T(1,128)S(1)}, f32[1,512]{1,0:T(1,128)}, u32[]{:S(2)}) copy-start(f32[1,512]{1,0:T(1,128)} %w_ref.3) | copy-start | bytes 6148
